TPU v7x, 1024 devices: a whole 4x8x16 slice. The times are simulated.
1024 devices in a mesh: dp: 32 (over y, x_hi, core), fsdp: 32 (over x_lo, z).
Axes of the slice: x: 4 (x_hi: 2, x_lo: 2; x = x_hi * 2 + x_lo), y: 8, z: 16, core: 2. Of those that a mesh axis runs over, the one named last changes fastest.
Arguments:
- grads: bfloat16 [32, 1024, 16384], P('dp', None, 'fsdp'), may hold values from -0.44 to 0.44
- stats: float32 [32, 32, 512, 512], P('dp', 'fsdp'), may hold values from -0.08 to 2, as said below
- left_root: bfloat16 [1024, 16384], P(None, 'fsdp'), may hold values from -0.02 to 1, as said below
- right_root: bfloat16 [1024, 16384], P(None, 'fsdp'), may hold values from -1.25 to 1.25, as said below
- owners: int32 [32, 2], replicated, may hold values from 0 to 31, as said below
Outputs:
- update: bfloat16 [1024, 16384], P(None, 'fsdp')
- new_stats: float32 [32, 32, 512, 512], P('dp', 'fsdp')
- new_root: bfloat16 [1024, 16384], P(None, 'fsdp')
Inputs may be any that keep to these rules, and one draw needn't show every extreme that they name: `stats`: symmetric in each slot. `left_root`: symmetric in each block. `right_root`: symmetric in each block. `owners`: the 2 entries of each row are distinct.
All inputs are finite; a program needn't handle non-finite values.
Results may differ from a plain program's by a relative error of at most 0.033.
Values may be sent and summed in bfloat16 or wider, within the bound.
No kernel may reach another device: no remote copies, remote signals or barrier semaphores. Data moves between devices by JAX's collectives and lax.ppermute only.
A program may use at most 32 MiB of HBM per device.

v0:
```python
import jax
import jax.numpy as jnp
from jax import lax
from jax.sharding import PartitionSpec as P

BETA = 0.95
EPSILON = 1e-06


def from_root(array, axis, root):
    mine = lax.axis_index(axis) == root
    return lax.psum(jnp.where(mine, array, jnp.zeros_like(array)), axis)


def precise(left_arg, right_arg):
    return jnp.dot(
        left_arg, right_arg, preferred_element_type=jnp.float32, precision=lax.Precision.HIGHEST
    )


def full_sum(local_grad):
    return lax.psum(local_grad.astype(jnp.float32).astype(jnp.bfloat16), "dp")


def local(grads, stats, left_root, right_root, owners):
    block_width = stats.shape[-1]
    block_rows = left_root.shape[0] // block_width
    replica = lax.axis_index("dp")
    column = lax.axis_index("fsdp")
    owner_row = lax.dynamic_index_in_dim(owners, column, 0, keepdims=False)
    owned_mask = owner_row == replica
    has_block = jnp.any(owned_mask)
    owned_index = jnp.sum(jnp.where(owned_mask, jnp.arange(block_rows, dtype=jnp.int32), 0))
    local_grad = grads[0]
    summed = None
    summed = full_sum(local_grad)
    grad_block = lax.dynamic_slice_in_dim(summed, owned_index * block_width, block_width, 0)
    left_block = lax.dynamic_slice_in_dim(left_root, owned_index * block_width, block_width, 0)
    right_block = lax.dynamic_slice_in_dim(right_root, owned_index * block_width, block_width, 0)
    old_stats = stats[0, 0]

    def fresh_owned():
        outer = lax.dot_general(
            grad_block, grad_block, (((1,), (1,)), ((), ())), preferred_element_type=jnp.float32
        )
        return BETA * old_stats + (1.0 - BETA) * outer

    def fresh_empty():
        return jnp.zeros_like(old_stats)

    fresh_stats = lax.cond(has_block, fresh_owned, fresh_empty)

    def newton_owned():
        start_root = left_block.astype(jnp.float32)
        square = precise(start_root, start_root)
        middle = precise(precise(square, fresh_stats), square)
        identity = jnp.eye(block_width, dtype=jnp.float32)
        return precise(start_root, (5.0 * identity - middle) * 0.25).astype(jnp.bfloat16)

    def newton_empty():
        return jnp.zeros((block_width, block_width), jnp.bfloat16)

    update_pieces = []
    root_pieces = []

    def precondition_owned():
        left_product = jnp.dot(left_block, grad_block, preferred_element_type=jnp.float32).astype(
            jnp.bfloat16
        )
        raw_update = jnp.dot(left_product, right_block, preferred_element_type=jnp.float32)
        return (raw_update.astype(jnp.bfloat16), jnp.sum(raw_update * raw_update))

    def precondition_empty():
        return (jnp.zeros((block_width, block_width), jnp.bfloat16), jnp.zeros((), jnp.float32))

    rounded, squares = lax.cond(has_block, precondition_owned, precondition_empty)
    root_new = lax.cond(has_block, newton_owned, newton_empty)
    for block_index in range(block_rows):
        got_update, got_root = (
            from_root(rounded, "dp", owner_row[block_index]),
            from_root(root_new, "dp", owner_row[block_index]),
        )
        update_pieces.append(got_update)
        root_pieces.append(got_root)
    total_squares = lax.psum(squares, ("dp", "fsdp"))
    rms_scale = lax.rsqrt(
        total_squares / (left_root.shape[0] * block_width * lax.axis_size("fsdp")) + EPSILON
    )
    scaled = [
        (piece.astype(jnp.float32) * rms_scale).astype(jnp.bfloat16) for piece in update_pieces
    ]
    update = jnp.concatenate(scaled, axis=0)
    new_root = jnp.concatenate(root_pieces, axis=0)
    new_stats = fresh_stats[None, None]
    return (update, new_stats, new_root)


def solution(mesh):
    in_specs = (
        P("dp", None, "fsdp"),
        P("dp", "fsdp", None, None),
        P(None, "fsdp"),
        P(None, "fsdp"),
        P(),
    )
    out_specs = (P(None, "fsdp"), P("dp", "fsdp", None, None), P(None, "fsdp"))
    return jax.shard_map(local, mesh=mesh, in_specs=in_specs, out_specs=out_specs, check_vma=False)
```

profile of v0, /device:TPU:1, one launch (start us, length us, event | category | flops | bytes accessed | tf_op | source)
XLA Modules:
  0.0 624.2 jit_solution(12753840859306721564)
XLA Ops:
  7.2 0.7 all-reduce.4.cloned.1.call-update
  8.0 0.7 fusion.6
  8.7 0.6 select_reduce_fusion
  10.6 0.5 fusion.8
  12.5 294.1 %all-reduce.4.cloned.1.call-done = bf16[1024,512]{1,0:T(8,128)(2,1)} async-done(((bf16[1024,512]{1,0:T(8,128)(2,1)}), bf16[1024,512]{1,0:T(8,128)(2,1)}) %all-reduce.4.cloned.1.call-update) | async-done | bytes 1048592 | tf_op jit(solution)/shard_map/psum | solution.py:22
  306.6 1.1 constant_dynamic-slice_fusion
  307.7 2.7 conditional.4
  307.8 1.4 fusion.3
  309.2 1.2 copy.22
  310.4 1.0 copy-done.2
  311.4 7.4 %conditional.5 = (bf16[512,512]{1,0:T(8,128)(2,1)S(1)}) conditional(s32[]{:T(128)} %convert_element_type.35, () %tuple.38, (bf16[512,512]{1,0:T(8,128)(2,1)S(1)}, f32[512,512]{1,0:T(8,128)}) %tuple.39), branch_computations={%region_11.12_spmd, %region_12.13_spmd} | conditional | flops 5101584384 | bytes 11010056 | solution.py:77
  311.4 0.4 fusion.9
  311.8 3.1 fusion.10
  314.9 1.8 fusion.4
  316.8 1.9 fusion.5
  318.8 3.1 conditional.3
  318.9 2.5 multiply_reduce_fusion
  321.9 1.1 broadcast_select_fusion.2
  323.0 1.0 broadcast_select_fusion.3
  324.1 122.9 %psum.44 = f32[]{:T(128)} all-reduce(f32[]{:T(128)} %get-tuple-element.48), channel_id=1, replica_groups=mesh['dp'=32,'fsdp'=32] {'dp','fsdp'}, use_global_device_ids=true, to_apply=%region_7.8 | all-reduce | flops 1 | bytes 8 | tf_op jit(solution)/shard_map/psum | solution.py:85
  447.7 166.1 %all-reduce.6.cloned.1.call-done = (bf16[512,512]{1,0:T(8,128)(2,1)}, bf16[512,512]{1,0:T(8,128)(2,1)}, bf16[512,512]{1,0:T(8,128)(2,1)}, bf16[512,512]{1,0:T(8,128)(2,1)}) async-done(((bf16[512,512]{1,0:T(8,128)(2,1)}, bf16[512,512]{1,0:T(8,128)(2,1)}, bf16[512,512]{1,0:T(8,128)(2,1)}, bf16[512,512]{1,0:T(8,128)(2,1)}), (bf16[512,512]{1,0:T(8,128)(2,1)}, bf16[512,512]{1,0:T(8,128)(2,1)}, ...) | async-done | bytes 2097168 | tf_op jit(solution)/shard_map/psum | solution.py:12
  613.8 2.3 pad_maximum_fusion.1
  616.1 0.2 multiply_convert_fusion
  616.4 1.0 pad_maximum_fusion
  (16 shorter events, 0.4 us)
Async XLA Ops:
  7.2 5.3 copy-start
  7.2 0.8 copy-start.5
  7.2 299.5 %all-reduce.4.cloned.1.call-start = ((), (), s32[]{:S(2)}) async-start(), calls=%async_computation | async-start | bytes 2097152 | tf_op jit(solution)/shard_map/psum | solution.py:22
  7.9 605.9 %all-reduce.6.cloned.1.call-start = ((), (), s32[]{:S(2)}) async-start(), calls=%async_computation.1 | async-start | bytes 4194304 | tf_op jit(solution)/shard_map/psum | solution.py:12
  12.5 295.3 %copy-start.1 = (f32[1,1,512,512]{3,2,1,0:T(8,128)S(1)}, f32[1,1,512,512]{3,2,1,0:T(8,128)}, u32[]{:S(2)}) copy-start(f32[1,1,512,512]{3,2,1,0:T(8,128)} %param.12) | copy-start | bytes 3145732
  310.4 1.0 copy-start.2
  613.8 2.3 copy-start.3
  613.8 2.3 copy-start.4
Sparse Core Ops, SparseCore 0:
  11.5 295.0 all-reduce.3
  324.2 289.5 all-reduce.5
where the time goes:
time: 625 us; the launch traced here: 624 us
  waiting for transfers between devices  461 us (74%)
  blocking collectives  123 us (20%)
  between operations  17.5 us (3%)
  matrix products  11.2 us (2%)
  other arithmetic  7.02 us (1%)
    psum x1, waiting for transfers between devices, full_sum(): return lax.psum(local_grad.astype(jnp.float32).astype(jnp.bfloat16), 'dp')  294 us
    psum x1, waiting for transfers between devices, from_root(): return lax.psum(jnp.where(mine, array, jnp.zeros_like(array)), axis)  166 us
    psum x1, blocking collectives, local(): total_squares = lax.psum(squares, ('dp', 'fsdp'))  123 us
  transfers between devices with their start and end apart: 2, of which 2 were waited for; matrix products, arithmetic and copies ran while one was open for 0% of the time, Pallas kernels for 0%

commit v1 on v0

v1 whole, which is shorter than its diff:
```python
import jax
import jax.numpy as jnp
from jax import lax
from jax.sharding import PartitionSpec as P

BETA = 0.95
EPSILON = 1e-06
F32 = jnp.float32
BF16 = jnp.bfloat16


def exchange(array, axis, groups=None):
    return lax.all_to_all(array, axis, 0, 0, axis_index_groups=groups)


def mm(left_arg, right_arg):
    return jnp.dot(left_arg, right_arg, preferred_element_type=F32)


def local(grads, stats, left_root, right_root, owners):
    n_dp = lax.axis_size("dp")
    n_fsdp = lax.axis_size("fsdp")
    chips = n_dp // 2
    width = stats.shape[-1]
    block_rows = left_root.shape[0] // width
    piece = width // chips
    half = piece // 2
    pairs = [[2 * k, 2 * k + 1] for k in range(chips)]
    same_core = [[2 * k + core for k in range(chips)] for core in range(2)]
    replica = lax.axis_index("dp")
    column = lax.axis_index("fsdp")
    owner_row = lax.dynamic_index_in_dim(owners, column, 0, keepdims=False)
    old_stats = stats[0, 0]

    grad_pair = exchange(grads[0].reshape(2, width, width), "dp", pairs)
    stat_pair = exchange(old_stats.astype(BF16).reshape(2, width // 2, width), "dp", pairs)
    grad_part = (grad_pair[0].astype(F32) + grad_pair[1].astype(F32)).astype(BF16)

    stat_pieces = stat_pair.reshape(2, chips, half, width).transpose(1, 0, 2, 3).reshape(chips, piece, width)
    sent = jnp.concatenate([grad_part.reshape(chips, piece, width), stat_pieces], axis=1)
    got = exchange(sent, "dp", same_core)
    grad_piece = jnp.sum(got[:, :piece].astype(F32), axis=0).astype(BF16)
    by_owner = got[:, piece:].reshape(n_dp, half, width)
    stat_piece = [
        lax.dynamic_index_in_dim(by_owner, owner_row[i], 0, keepdims=False) for i in range(block_rows)
    ]

    whole = jnp.concatenate([grad_piece, *stat_piece], axis=0)
    mine = exchange(jnp.broadcast_to(whole[None], (chips, *whole.shape)), "dp", same_core)
    other = lax.ppermute(mine, "dp", [(k, k ^ 1) for k in range(n_dp)])
    first = lax.rem(replica, 2) == 0
    of_core = (jnp.where(first, mine, other), jnp.where(first, other, mine))

    rounded = []
    roots = []
    grams = []
    squares = jnp.zeros((), F32)
    for i in range(block_rows):
        grad_block = of_core[i][:, :piece].reshape(width, width)
        left = left_root[i * width : (i + 1) * width]
        right = right_root[i * width : (i + 1) * width]
        raw = mm(mm(left, grad_block).astype(BF16), right)
        squares = squares + jnp.sum(raw * raw)
        rounded.append(raw.astype(BF16))
        gram = lax.dot_general(grad_block, grad_block, (((1,), (1,)), ((), ())), preferred_element_type=F32)
        grams.append(gram)
        start = piece + i * half
        stat_block = jnp.concatenate(
            [part[:, start : start + half].reshape(width // 2, width) for part in of_core], axis=0
        )
        fresh = (BETA * stat_block.astype(F32) + (1.0 - BETA) * gram).astype(BF16)
        square = mm(left, left).astype(BF16)
        cube = mm(left, square).astype(BF16)
        roots.append(
            (1.25 * left.astype(F32) - 0.25 * mm(cube, mm(fresh, square).astype(BF16))).astype(BF16)
        )

    every = exchange(jnp.broadcast_to(squares, (n_fsdp, 1, 128)), "fsdp")
    total = jnp.sum(every[:, 0, 0])
    scale = lax.rsqrt(total / (left_root.shape[0] * width * n_fsdp) + EPSILON)
    update = jnp.concatenate([(piece_.astype(F32) * scale).astype(BF16) for piece_ in rounded], axis=0)
    new_root = jnp.concatenate(roots, axis=0)
    mine_gram = grams[0]
    has_block = owner_row[0] == replica
    for i in range(1, block_rows):
        mine_gram = jnp.where(owner_row[i] == replica, grams[i], mine_gram)
        has_block = has_block | (owner_row[i] == replica)
    new_stats = jnp.where(has_block, BETA * old_stats + (1.0 - BETA) * mine_gram, 0.0)
    return (update, new_stats[None, None], new_root)


def solution(mesh):
    in_specs = (
        P("dp", None, "fsdp"),
        P("dp", "fsdp", None, None),
        P(None, "fsdp"),
        P(None, "fsdp"),
        P(),
    )
    out_specs = (P(None, "fsdp"), P("dp", "fsdp", None, None), P(None, "fsdp"))
    return jax.shard_map(local, mesh=mesh, in_specs=in_specs, out_specs=out_specs, check_vma=False)
```

time: 625 us -> 151 us (0.24)
  waiting for transfers between devices: 461 us -> 34.5 us
  blocking collectives: 123 us -> 51.9 us
  starting transfers between devices: 0.08 us -> 24.4 us
  between operations: 17.5 us -> 7.9 us
  matrix products: 11.2 us -> 20.6 us
    psum x2 -> x0, waiting for transfers between devices: 460 us -> none  [the longest x1 294 us: full_sum(): return lax.psum(local_grad.astype(jnp.float32).astype(jnp.bfloat16), 'dp')]
    psum x1 -> x0, blocking collectives: 123 us -> none  [local(): total_squares = lax.psum(squares, ('dp', 'fsdp'))]
    all_to_all x0 -> x2, blocking collectives: none -> 51.9 us  [exchange(): return lax.all_to_all(array, axis, 0, 0, axis_index_groups=groups)]
    all_to_all x0 -> x3, waiting for transfers between devices: none -> 34.5 us  [exchange(): return lax.all_to_all(array, axis, 0, 0, axis_index_groups=groups)]
    all_to_all x0 -> x3, starting transfers between devices: none -> 19.9 us  [exchange(): return lax.all_to_all(array, axis, 0, 0, axis_index_groups=groups)]
    dot_general x6 -> x10, matrix products: 11.2 us -> 20.6 us  [the longest x8 19.7 us: mm(): return jnp.dot(left_arg, right_arg, preferred_element_type=F32)]
  transfers between devices with their start and end apart: 2 -> 4, of which waited for: 2 -> 3; matrix products, arithmetic and copies ran while one was open for 0% -> 4% of each run, Pallas kernels for 0% -> 0%
where the time goes in v1:
time: 151 us; the launch traced here: 150 us
  blocking collectives  51.9 us (34%)
  waiting for transfers between devices  34.5 us (23%)
  starting transfers between devices  24.4 us (16%)
  matrix products  20.6 us (14%)
  other arithmetic  8.32 us (6%)
  between operations  7.9 us (5%)
  local copies, waits for them, and re-layouts  2.37 us (2%)
    all_to_all x2, blocking collectives, exchange(): return lax.all_to_all(array, axis, 0, 0, axis_index_groups=groups)  51.9 us
    all_to_all x3, waiting for transfers between devices, exchange(): return lax.all_to_all(array, axis, 0, 0, axis_index_groups=groups)  34.5 us
    all_to_all x3, starting transfers between devices, exchange(): return lax.all_to_all(array, axis, 0, 0, axis_index_groups=groups)  19.9 us
    dot_general x8, matrix products, mm(): return jnp.dot(left_arg, right_arg, preferred_element_type=F32)  19.7 us
    ppermute x1, starting transfers between devices, local(): other = lax.ppermute(mine, 'dp', [(k, k ^ 1) for k in range(n_dp)])  4.46 us
  transfers between devices with their start and end apart: 4, of which 3 were waited for; matrix products, arithmetic and copies ran while one was open for 4% of the time, Pallas kernels for 0%

profile of v1, /device:TPU:1, one launch (start us, length us, event | category | flops | bytes accessed | tf_op | source)
XLA Modules:
  0.0 150.0 jit_solution(15161846310739337860)
XLA Ops:
  0.6 1.3 convert_element_type.100
  1.9 17.9 %all_to_all.25 = bf16[2,256,512]{2,1,0:T(8,128)(2,1)S(1)} all-to-all(bf16[2,256,512]{2,1,0:T(8,128)(2,1)S(1)} %bitcast.44), channel_id=1, replica_groups={{0,32},{64,96},{128,160},{192,224},{256,288},{320,352},{384,416},{448,4..., dimensions={0} | all-to-all | bytes 1048576 | tf_op jit(solution)/shard_map/all_to_all | solution.py:13
  19.9 3.9 %all-to-all-start = ((bf16[2,512,512]{2,1,0:T(8,128)(2,1)}), bf16[2,512,512]{2,1,0:T(8,128)(2,1)S(1)}, u32[]{:S(2)}, u32[]{:S(2)}) async-start(bf16[2,512,512]{2,1,0:T(8,128)(2,1)} %bitcast), calls=%async_computation | async-start | bytes 2097152 | tf_op jit(solution)/shard_map/all_to_all | solution.py:13
  23.9 1.7 %all-to-all-done = bf16[2,512,512]{2,1,0:T(8,128)(2,1)S(1)} async-done(((bf16[2,512,512]{2,1,0:T(8,128)(2,1)}), bf16[2,512,512]{2,1,0:T(8,128)(2,1)S(1)}, u32[]{:S(2)}, u32[]{:S(2)}) %all-to-all-start) | async-done | bytes 1048608 | tf_op jit(solution)/shard_map/all_to_all | solution.py:13
  25.7 1.1 pad_maximum_fusion
  26.8 3.7 %all-to-all-start.2 = ((bf16[16,64,512]{2,1,0:T(8,128)(2,1)}), bf16[16,64,512]{2,1,0:T(8,128)(2,1)S(1)}, u32[]{:S(2)}, u32[]{:S(2)}) async-start(bf16[16,64,512]{2,1,0:T(8,128)(2,1)} %pad_maximum_fusion), calls=%async_computation.2 | async-start | bytes 2097152 | tf_op jit(solution)/shard_map/all_to_all | solution.py:13
  34.9 22.9 %all-to-all-done.2 = bf16[16,64,512]{2,1,0:T(8,128)(2,1)S(1)} async-done(((bf16[16,64,512]{2,1,0:T(8,128)(2,1)}), bf16[16,64,512]{2,1,0:T(8,128)(2,1)S(1)}, u32[]{:S(2)}, u32[]{:S(2)}) %all-to-all-start.2) | async-done | bytes 1048608 | tf_op jit(solution)/shard_map/all_to_all | solution.py:13
  58.1 33.9 %all_to_all.26 = bf16[16,64,512]{2,1,0:T(8,128)(2,1)S(1)} all-to-all(bf16[16,64,512]{2,1,0:T(8,128)(2,1)S(1)} %broadcast_in_dim.16), channel_id=1, replica_groups={{0,64,128,192,256,320,384,448,512,576,640,704,768,832,896,960},{32,96,1..., dimensions={0} | all-to-all | bytes 2097152 | tf_op jit(solution)/shard_map/all_to_all | solution.py:13
  92.1 4.5 %collective-permute-start = (bf16[16,64,512]{2,1,0:T(8,128)(2,1)S(1)}, bf16[16,64,512]{2,1,0:T(8,128)(2,1)S(1)}, u32[]{:S(2)}, u32[]{:S(2)}) collective-permute-start(bf16[16,64,512]{2,1,0:T(8,128)(2,1)S(1)} %all_to_all.26), channel_id=1, source_target_pairs={{0,32},{32,0},{64,96},{96,64},{128,160},{160,128},{192,224},{224,1... | collective-permute-start | bytes 3145736 | tf_op jit(solution)/shard_map/ppermute | solution.py:50
  97.9 1.2 convolution_convert_fusion.5
  99.1 1.2 convolution_convert_fusion.2
  100.5 0.9 fusion.36
  102.4 3.5 %multiply_reduce_fusion.1 = (f32[]{:T(128)}, bf16[512,512]{1,0:T(8,128)(2,1)}) fusion(bf16[1024,512]{1,0:T(8,128)(2,1)} %param.8, bf16[512,512]{1,0:T(8,128)(2,1)S(1)} %bitcast.41, bf16[1024,512]{1,0:T(8,128)(2,1)} %param.7), kind=kOutput, calls=%fused_computation.27 | convolution fusion | flops 537919488 | bytes 2097156 | tf_op jit(solution)/shard_map/dot_general | solution.py:17
  105.9 3.6 %multiply_reduce_fusion = (f32[]{:T(128)}, bf16[512,512]{1,0:T(8,128)(2,1)}) fusion(bf16[1024,512]{1,0:T(8,128)(2,1)} %param.8, bf16[512,512]{1,0:T(8,128)(2,1)S(1)} %bitcast.43, bf16[1024,512]{1,0:T(8,128)(2,1)} %param.7), kind=kOutput, calls=%fused_computation.26 | convolution fusion | flops 537919488 | bytes 2097156 | tf_op jit(solution)/shard_map/dot_general | solution.py:17
  109.6 2.3 %convolution_convert_fusion.3 = bf16[512,512]{1,0:T(8,128)(2,1)} fusion(bf16[512,512]{1,0:T(8,128)(2,1)} %convolution_convert_fusion.5, f32[512,512]{1,0:T(8,128)S(1)} %fusion.44, bf16[256,512]{1,0:T(8,128)(2,1)S(1)} %bitcast.52, bf16[256,512]{1,0:T(8,128)(2,1)S(1)} %bitcast.51), kind=kOutput, calls=%fused_computation.9 | convolution fusion | flops 270794752 | bytes 2621440 | tf_op jit(solution)/shard_map/dot_general | solution.py:17
  111.9 3.2 %fusion.2 = bf16[512,512]{1,0:T(8,128)(2,1)} fusion(bf16[512,512]{1,0:T(8,128)(2,1)} %convolution_convert_fusion.3, bf16[512,512]{1,0:T(8,128)(2,1)} %convolution_convert_fusion.5, bf16[1024,512]{1,0:T(8,128)(2,1)} %param.7), kind=kOutput, calls=%fused_computation.4 | convolution fusion | flops 538443776 | bytes 2621440 | tf_op jit(solution)/shard_map/dot_general | solution.py:17
  115.1 1.2 convolution_convert_fusion
  116.4 3.3 %fusion.3 = bf16[512,512]{1,0:T(8,128)(2,1)} fusion(bf16[512,512]{1,0:T(8,128)(2,1)} %convolution_convert_fusion, bf16[512,512]{1,0:T(8,128)(2,1)} %convolution_convert_fusion.2, bf16[1024,512]{1,0:T(8,128)(2,1)} %param.7), kind=kOutput, calls=%fused_computation.5 | convolution fusion | flops 538443776 | bytes 2621440 | tf_op jit(solution)/shard_map/dot_general | solution.py:17
  119.7 1.3 fusion.7
  122.8 12.3 %all-to-all-start.4 = ((f32[32,1,128]{2,1,0:T(1,128)}), f32[32,1,128]{2,1,0:T(1,128)S(1)}, u32[]{:S(2)}, u32[]{:S(2)}) async-start(f32[32,1,128]{2,1,0:T(1,128)} %broadcast_in_dim.17), calls=%async_computation.4 | async-start | bytes 32768 | tf_op jit(solution)/shard_map/all_to_all | solution.py:13
  135.2 2.3 %pad_maximum_fusion.2 = bf16[1024,512]{1,0:T(8,128)(2,1)} fusion(bf16[512,512]{1,0:T(8,128)(2,1)} %fusion.3, bf16[512,512]{1,0:T(8,128)(2,1)} %fusion.2), kind=kLoop, calls=%fused_computation.18 | loop fusion | flops 2097152 | bytes 2097152 | tf_op jit(solution)/shard_map/concatenate | solution.py:82
  137.5 9.8 %all-to-all-done.4 = f32[32,1,128]{2,1,0:T(1,128)S(1)} async-done(((f32[32,1,128]{2,1,0:T(1,128)}), f32[32,1,128]{2,1,0:T(1,128)S(1)}, u32[]{:S(2)}, u32[]{:S(2)}) %all-to-all-start.4) | async-done | bytes 16416 | tf_op jit(solution)/shard_map/all_to_all | solution.py:13
  147.4 0.6 slice_reduce_fusion.1
  148.9 1.0 pad_maximum_fusion.1
  (34 shorter events, 3.0 us)
Async XLA Ops:
  0.6 29.8 %copy-start = (s32[32,2]{0,1:T(2,128)S(1)}, s32[32,2]{0,1:T(2,128)}, u32[]{:S(2)}) copy-start(s32[32,2]{0,1:T(2,128)} %param.9) | copy-start | bytes 772
  19.9 5.7 %all-to-all-start = ((bf16[2,512,512]{2,1,0:T(8,128)(2,1)}), bf16[2,512,512]{2,1,0:T(8,128)(2,1)S(1)}, u32[]{:S(2)}, u32[]{:S(2)}) async-start(bf16[2,512,512]{2,1,0:T(8,128)(2,1)} %bitcast), calls=%async_computation | async-start | bytes 2097152 | tf_op jit(solution)/shard_map/all_to_all | solution.py:13
  26.8 31.1 %all-to-all-start.2 = ((bf16[16,64,512]{2,1,0:T(8,128)(2,1)}), bf16[16,64,512]{2,1,0:T(8,128)(2,1)S(1)}, u32[]{:S(2)}, u32[]{:S(2)}) async-start(bf16[16,64,512]{2,1,0:T(8,128)(2,1)} %pad_maximum_fusion), calls=%async_computation.2 | async-start | bytes 2097152 | tf_op jit(solution)/shard_map/all_to_all | solution.py:13
  58.1 39.7 %copy-start.7 = (bf16[1024,512]{1,0:T(8,128)(2,1)S(1)}, bf16[1024,512]{1,0:T(8,128)(2,1)}, u32[]{:S(2)}) copy-start(bf16[1024,512]{1,0:T(8,128)(2,1)} %param.7) | copy-start | bytes 3145732
  92.1 8.2 %collective-permute-start = (bf16[16,64,512]{2,1,0:T(8,128)(2,1)S(1)}, bf16[16,64,512]{2,1,0:T(8,128)(2,1)S(1)}, u32[]{:S(2)}, u32[]{:S(2)}) collective-permute-start(bf16[16,64,512]{2,1,0:T(8,128)(2,1)S(1)} %all_to_all.26), channel_id=1, source_target_pairs={{0,32},{32,0},{64,96},{96,64},{128,160},{160,128},{192,224},{224,1... | collective-permute-start | bytes 3145736 | tf_op jit(solution)/shard_map/ppermute | solution.py:50
  105.9 3.7 %copy-start.5 = (bf16[16,16,512]{2,1,0:T(8,128)(2,1)S(1)}, bf16[16,16,512]{2,1,0:T(8,128)(2,1)}, u32[]{:S(2)}) copy-start(bf16[16,16,512]{2,1,0:T(8,128)(2,1)} %get-tuple-element.5) | copy-start | bytes 786436
  105.9 3.7 %copy-start.6 = (bf16[16,16,512]{2,1,0:T(8,128)(2,1)S(1)}, bf16[16,16,512]{2,1,0:T(8,128)(2,1)}, u32[]{:S(2)}) copy-start(bf16[16,16,512]{2,1,0:T(8,128)(2,1)} %get-tuple-element.20) | copy-start | bytes 786436
  111.9 3.2 %copy-start.4 = (bf16[16,16,512]{2,1,0:T(8,128)(2,1)S(1)}, bf16[16,16,512]{2,1,0:T(8,128)(2,1)}, u32[]{:S(2)}) copy-start(bf16[16,16,512]{2,1,0:T(8,128)(2,1)} %get-tuple-element.19) | copy-start | bytes 786436
  111.9 3.2 %copy-start.8 = (bf16[512,512]{1,0:T(8,128)(2,1)S(1)}, bf16[512,512]{1,0:T(8,128)(2,1)}, u32[]{:S(2)}) copy-start(bf16[512,512]{1,0:T(8,128)(2,1)} %convolution_convert_fusion.2) | copy-start | bytes 1572868
  116.4 3.3 %copy-start.1 = (f32[1,1,512,512]{3,2,1,0:T(8,128)S(1)}, f32[1,1,512,512]{3,2,1,0:T(8,128)}, u32[]{:S(2)}) copy-start(f32[1,1,512,512]{3,2,1,0:T(8,128)} %param.6) | copy-start | bytes 3145732
  122.8 24.5 %all-to-all-start.4 = ((f32[32,1,128]{2,1,0:T(1,128)}), f32[32,1,128]{2,1,0:T(1,128)S(1)}, u32[]{:S(2)}, u32[]{:S(2)}) async-start(f32[32,1,128]{2,1,0:T(1,128)} %broadcast_in_dim.17), calls=%async_computation.4 | async-start | bytes 32768 | tf_op jit(solution)/shard_map/all_to_all | solution.py:13
  135.2 13.5 %copy-start.2 = (bf16[512,512]{1,0:T(8,128)(2,1)S(1)}, bf16[512,512]{1,0:T(8,128)(2,1)}, u32[]{:S(2)}) copy-start(bf16[512,512]{1,0:T(8,128)(2,1)} %get-tuple-element.16) | copy-start | bytes 1572868
  135.2 13.5 %copy-start.3 = (bf16[512,512]{1,0:T(8,128)(2,1)S(1)}, bf16[512,512]{1,0:T(8,128)(2,1)}, u32[]{:S(2)}) copy-start(bf16[512,512]{1,0:T(8,128)(2,1)} %get-tuple-element.18) | copy-start | bytes 1572868

commit v2 on v1

v2 whole, which is shorter than its diff:
```python
import jax
import jax.numpy as jnp
from jax import lax
from jax.experimental import pallas as pl
from jax.experimental.pallas import tpu as pltpu
from jax.sharding import PartitionSpec as P

BETA = 0.95
EPSILON = 1e-06
F32 = jnp.float32
BF16 = jnp.bfloat16

WIDTH = 512
HALF = 256
TILE = 128
SLOT = 32
CHIPS = 16
N_DP = 32
FIRST = TILE + 2 * SLOT + 16
SECOND = TILE + 2 * SLOT


def exchange(array, axis, groups=None):
    return lax.all_to_all(array, axis, 0, 0, axis_index_groups=groups)


def mm(left_arg, right_arg):
    return jnp.dot(left_arg, right_arg, preferred_element_type=F32)


def row_col(rows, cols):
    shape = (rows, cols)
    return lax.broadcasted_iota(jnp.int32, shape, 0), lax.broadcasted_iota(jnp.int32, shape, 1)


def call(body, meta, args, outs, flops, scratch=()):
    vmem = pl.BlockSpec(memory_space=pltpu.VMEM)
    moved = sum(a.size * a.dtype.itemsize for a in args) + sum(o.size * o.dtype.itemsize for o in outs)
    return pl.pallas_call(
        body,
        out_shape=outs,
        in_specs=[pl.BlockSpec(memory_space=pltpu.SMEM)] + [vmem] * len(args),
        out_specs=[vmem] * len(outs),
        scratch_shapes=scratch,
        cost_estimate=pl.CostEstimate(flops=flops, bytes_accessed=moved, transcendentals=0),
        compiler_params=pltpu.CompilerParams(vmem_limit_bytes=16 << 20),
    )(meta, *args)


def pack(meta, grads, stats, send, keep):
    core = meta[0]
    other = 1 - core
    send[0:WIDTH] = grads[0, pl.ds(pl.multiple_of(other * WIDTH, WIDTH), WIDTH)]
    row, col = row_col(HALF, HALF)
    low = stats[0, 0, HALF:, HALF:]
    both = jnp.where(row <= col, stats[0, 0, :HALF, :HALF], low).astype(BF16)
    corner = stats[0, 0, :HALF, HALF:].astype(BF16)
    diagonal = jnp.sum(jnp.where(row == col, low, 0.0), axis=0, keepdims=True)
    line, _ = row_col(16, TILE)
    lines = jnp.where(line == 8 * core, diagonal[:, :TILE], jnp.where(line == 8 * core + 1, diagonal[:, TILE:], 0.0))
    lines = lines.astype(BF16)

    @pl.when(core == 0)
    def _():
        keep[0:TILE, :HALF] = corner[:TILE]
        keep[0:TILE, HALF:] = both[:TILE]
        send[WIDTH : WIDTH + TILE, :HALF] = corner[TILE:]
        send[WIDTH : WIDTH + TILE, HALF:] = both[TILE:]

    @pl.when(core == 1)
    def _():
        keep[0:TILE, :HALF] = corner[TILE:]
        keep[0:TILE, HALF:] = both[TILE:]
        send[WIDTH : WIDTH + TILE, :HALF] = corner[:TILE]
        send[WIDTH : WIDTH + TILE, HALF:] = both[:TILE]

    for start in range(0, WIDTH, TILE):
        keep[TILE:, start : start + TILE] = lines
        send[WIDTH + TILE :, start : start + TILE] = lines


def pair_add(meta, grads, keep, got, out):
    core = meta[0]
    base = core * WIDTH
    mine = pl.multiple_of(TILE + SLOT * core, SLOT)
    theirs = pl.multiple_of(TILE + SLOT * (1 - core), SLOT)
    lines = (keep[TILE:, :TILE].astype(F32) + got[WIDTH + TILE :, :TILE].astype(F32)).astype(BF16)
    for chip in range(CHIPS):
        cols = slice(TILE * (chip // 4), TILE * (chip // 4) + TILE)
        top = TILE * (chip % 4)
        own = grads[0, pl.ds(pl.multiple_of(base + top, TILE), TILE), cols].astype(F32)
        out[chip, 0:TILE] = (own + got[top : top + TILE, cols].astype(F32)).astype(BF16)
        at = SLOT * (chip % 4)
        out[chip, pl.ds(mine, SLOT)] = keep[at : at + SLOT, cols]
        out[chip, pl.ds(theirs, SLOT)] = got[WIDTH + at : WIDTH + at + SLOT, cols]
        out[chip, SECOND:] = lines


def gather_sum(meta, got, out, diagonals):
    total = got[0, 0:TILE].astype(F32)
    for chip in range(1, CHIPS):
        total = total + got[chip, 0:TILE].astype(F32)
    total = total.astype(BF16)
    line, _ = row_col(16, TILE)
    lines = jnp.zeros((16, TILE), F32)
    slots = []
    for i in range(2):
        owner = meta[1 + i]
        chip = owner // 2
        side = owner % 2
        slots.append(got[chip, pl.ds(pl.multiple_of(TILE + SLOT * side, SLOT), SLOT)])
        rows = got[chip, SECOND:].astype(F32)
        pick = jnp.where(side == 0, rows[0:8], rows[8:16])
        lines = jnp.where(line == 8 * i, pick[0:1], jnp.where(line == 8 * i + 1, pick[1:2], lines))
    diagonals[...] = lines
    for chip in range(CHIPS):
        out[chip, 0:TILE] = total
        for i in range(2):
            out[chip, TILE + SLOT * i : TILE + SLOT * (i + 1)] = slots[i]


def load_grad(source, grad):
    for chip in range(CHIPS):
        top = TILE * (chip % 4)
        left = TILE * (chip // 4)
        grad[top : top + TILE, left : left + TILE] = source[chip, 0:TILE]


def precondition(meta, mine, other, left_root, right_root, rounded, squares, grad):
    core = meta[0]
    total = jnp.zeros((1, 1), F32)
    for source, block in ((mine, core), (other, 1 - core)):
        rows = pl.ds(pl.multiple_of(block * WIDTH, WIDTH), WIDTH)
        load_grad(source, grad)
        product = mm(left_root[rows, :], grad[...]).astype(BF16)
        raw = mm(product, right_root[rows, :])
        rounded[rows, :] = raw.astype(BF16)
        column = jnp.sum(raw * raw, axis=0, keepdims=True)
        total = total + jnp.sum(column, axis=1, keepdims=True)
    filled = jnp.broadcast_to(total, squares.shape[1:])
    for k in range(squares.shape[0]):
        squares[k] = filled


def newton(meta, mine, other, diagonals, left_root, stats, squares, new_root, new_stats, grad):
    core = meta[0]
    owner_known = (meta[1] == meta[3]) | (meta[2] == meta[3])
    row, col = row_col(HALF, HALF)

    @pl.when(jnp.logical_not(owner_known))
    def _():
        new_stats[...] = jnp.zeros_like(new_stats)

    def one(block, source, first, second):
        rows = slice(block * WIDTH, (block + 1) * WIDTH)
        load_grad(source, grad)
        gram = lax.dot_general(
            grad[...], grad[...], (((1,), (1,)), ((), ())), preferred_element_type=F32
        )

        @pl.when(meta[1 + block] == meta[3])
        def _():
            new_stats[0, 0] = BETA * stats[0, 0] + (1.0 - BETA) * gram

        start = TILE + SLOT * block

        def panel(part, k):
            return part[4 * k : 4 * k + 4, start : start + SLOT].reshape(TILE, TILE)

        packed = [
            jnp.concatenate(
                [jnp.concatenate([panel(part, k), panel(part, k + 1)], axis=1) for part in (first, second)], axis=0
            ).astype(F32)
            for k in (0, 2)
        ]
        corner, both = packed
        corner_t = jnp.transpose(corner)
        both_t = jnp.transpose(both)
        diagonal = jnp.concatenate(
            [diagonals[8 * block : 8 * block + 1], diagonals[8 * block + 1 : 8 * block + 2]], axis=1
        )
        high = jnp.where(row <= col, both, both_t)
        low = jnp.where(row > col, both, jnp.where(row == col, diagonal, both_t))
        old = jnp.concatenate(
            [jnp.concatenate([high, corner], axis=1), jnp.concatenate([corner_t, low], axis=1)], axis=0
        )
        fresh = (BETA * old + (1.0 - BETA) * gram).astype(BF16)
        left = left_root[rows, :]
        square = mm(left, left).astype(BF16)
        cube = mm(left, square).astype(BF16)
        change = mm(cube, mm(fresh, square).astype(BF16))
        new_root[rows, :] = (1.25 * left.astype(F32) - 0.25 * change).astype(BF16)

    @pl.when(core == 0)
    def _():
        one(0, mine, mine, other)
        one(1, other, mine, other)

    @pl.when(core == 1)
    def _():
        one(0, other, other, mine)
        one(1, mine, other, mine)


def rescale(count):
    def body(meta, every, rounded, update):
        total = every[0]
        for k in range(1, every.shape[0]):
            total = total + every[k]
        scale = lax.rsqrt(total[0:1, 0:1] / count + EPSILON)
        update[...] = (rounded[...].astype(F32) * scale).astype(BF16)

    return body


def local(grads, stats, left_root, right_root, owners):
    n_fsdp = lax.axis_size("fsdp")
    rows = left_root.shape[0]
    same_core = [[2 * k + core for k in range(CHIPS)] for core in range(2)]
    swap = [(k, k ^ 1) for k in range(N_DP)]
    replica = lax.axis_index("dp")
    column = lax.axis_index("fsdp")
    owner_row = lax.dynamic_index_in_dim(owners, column, 0, keepdims=False)
    meta = jnp.stack([lax.rem(replica, 2), owner_row[0], owner_row[1], replica]).astype(jnp.int32)
    shape = jax.ShapeDtypeStruct
    product = 2 * WIDTH**3

    send, keep = call(
        pack,
        meta,
        [grads, stats],
        [shape((WIDTH + TILE + 16, WIDTH), BF16), shape((TILE + 16, WIDTH), BF16)],
        1 << 20,
    )
    got = lax.ppermute(send, "dp", swap)
    (payload,) = call(pair_add, meta, [grads, keep, got], [shape((CHIPS, FIRST, TILE), BF16)], 1 << 20)
    arrived = exchange(payload, "dp", same_core)
    repeated, diagonals = call(
        gather_sum,
        meta,
        [arrived],
        [shape((CHIPS, SECOND, TILE), BF16), shape((16, TILE), F32)],
        1 << 20,
    )
    mine = exchange(repeated, "dp", same_core)
    other = lax.ppermute(mine, "dp", swap)
    rounded, squares = call(
        precondition,
        meta,
        [mine, other, left_root, right_root],
        [shape((rows, WIDTH), BF16), shape((n_fsdp, 8, TILE), F32)],
        4 * product,
        [pltpu.VMEM((WIDTH, WIDTH), BF16)],
    )
    every = exchange(squares, "fsdp")
    new_root, new_stats = call(
        newton,
        meta,
        [mine, other, diagonals, left_root, stats, squares],
        [shape((rows, WIDTH), BF16), shape((1, 1, WIDTH, WIDTH), F32)],
        10 * product,
        [pltpu.VMEM((WIDTH, WIDTH), BF16)],
    )
    (update,) = call(rescale(float(rows * WIDTH * n_fsdp)), meta, [every, rounded], [shape((rows, WIDTH), BF16)], 1 << 20)
    return (update, new_stats, new_root)


def solution(mesh):
    in_specs = (
        P("dp", None, "fsdp"),
        P("dp", "fsdp", None, None),
        P(None, "fsdp"),
        P(None, "fsdp"),
        P(),
    )
    out_specs = (P(None, "fsdp"), P("dp", "fsdp", None, None), P(None, "fsdp"))
    return jax.shard_map(local, mesh=mesh, in_specs=in_specs, out_specs=out_specs, check_vma=False)
```

time: 151 us -> 120 us (0.79)
  waiting for transfers between devices: 34.5 us -> 10.3 us
  matrix products: 20.6 us -> 0 us
  Pallas kernels: 0 us -> 12.6 us
  starting transfers between devices: 24.4 us -> 33.8 us
  between operations: 7.9 us -> 0.72 us
  other arithmetic: 8.32 us -> 1.37 us
  local copies, waits for them, and re-layouts: 2.37 us -> 6.08 us
  blocking collectives: 51.9 us -> 54.3 us
    all_to_all x3 -> x1, waiting for transfers between devices: 34.5 us -> 6.7 us  [exchange(): return lax.all_to_all(array, axis, 0, 0, axis_index_groups=groups)]
    dot_general x10 -> x0, matrix products: 20.6 us -> none  [the longest x8 19.7 us: mm(): return jnp.dot(left_arg, right_arg, preferred_element_type=F32)]
    ppermute x1 -> x2, starting transfers between devices: 4.46 us -> 21 us  [the longest x1 16.1 us: local(): got = lax.ppermute(send, 'dp', swap)]
    pallas_call x0 -> x6, Pallas kernels: none -> 12.6 us  [call(): pl.pallas_call(body, out_shape=outs, in_specs=[pl.BlockSpec(memory_space=...]
    all_to_all x3 -> x1, starting transfers between devices: 19.9 us -> 12.8 us  [exchange(): return lax.all_to_all(array, axis, 0, 0, axis_index_groups=groups)]
    unnamed x18, local copies, waits for them, and re-layouts: 0.04 us -> 5.49 us
    concatenate x4 -> x0, other arithmetic: 4.43 us -> none  [the longest x1 2.32 us: local(): new_root = jnp.concatenate(roots, axis=0)]
    ppermute x1 -> x2, waiting for transfers between devices: 0.01 us -> 3.62 us  [the longest x1 1.89 us: local(): other = lax.ppermute(mine, 'dp', swap)]
  transfers between devices with their start and end apart: 4 -> 3, of which waited for: 3 -> 3; matrix products, arithmetic and copies ran while one was open for 4% -> 0% of each run, Pallas kernels for 0% -> 5%
where the time goes in v2:
time: 120 us; the launch traced here: 119 us
  blocking collectives  54.3 us (45%)
  starting transfers between devices  33.8 us (28%)
  Pallas kernels  12.6 us (10%)
  waiting for transfers between devices  10.3 us (9%)
  local copies, waits for them, and re-layouts  6.08 us (5%)
  other arithmetic  1.37 us (1%)
    all_to_all x2, blocking collectives, exchange(): return lax.all_to_all(array, axis, 0, 0, axis_index_groups=groups)  54.3 us
    ppermute x1, starting transfers between devices, local(): got = lax.ppermute(send, 'dp', swap)  16.1 us
    all_to_all x1, starting transfers between devices, exchange(): return lax.all_to_all(array, axis, 0, 0, axis_index_groups=groups)  12.8 us
    pallas_call x6, Pallas kernels, call(): pl.pallas_call(body, out_shape=outs, in_specs=[pl.BlockSpec(memory_space=...  12.6 us
    all_to_all x1, waiting for transfers between devices, exchange(): return lax.all_to_all(array, axis, 0, 0, axis_index_groups=groups)  6.7 us
    unnamed x18, local copies, waits for them, and re-layouts  5.49 us
    ppermute x1, starting transfers between devices, local(): other = lax.ppermute(mine, 'dp', swap)  4.89 us
  transfers between devices with their start and end apart: 3, of which 3 were waited for; matrix products, arithmetic and copies ran while one was open for 0% of the time, Pallas kernels for 5%

profile of v2, /device:TPU:1, one launch (start us, length us, event | category | flops | bytes accessed | tf_op | source)
XLA Modules:
  0.0 119.1 jit_solution(18247496119026702675)
XLA Ops:
  0.6 0.0 copy-start
  0.7 0.7 copy-done
  1.3 0.1 constant_dynamic-slice_fusion
  1.4 0.5 fusion
  1.9 1.4 %pad_add_fusion.meta = s32[4]{0:T(128)S(1)} fusion(s32[1]{0:T(128)} %bitcast.3, s32[1]{0:T(128)} %bitcast.2, s32[1]{0:T(128)} %bitcast.1, s32[1]{0:T(128)} %bitcast), kind=kLoop, calls=%fused_computation | loop fusion | flops 12 | bytes 32 | tf_op jit(solution)/shard_map/stack | solution.py:224
  3.3 1.2 %copy-done.1 = bf16[1,1024,512]{2,1,0:T(8,128)(2,1)S(1)} copy-done((bf16[1,1024,512]{2,1,0:T(8,128)(2,1)S(1)}, bf16[1,1024,512]{2,1,0:T(8,128)(2,1)}, u32[]{:S(2)}) %copy-start.1) | copy-done | bytes 1048600
  4.5 1.2 %copy-done.2 = f32[1,1,512,512]{3,2,1,0:T(8,128)S(1)} copy-done((f32[1,1,512,512]{3,2,1,0:T(8,128)S(1)}, f32[1,1,512,512]{3,2,1,0:T(8,128)}, u32[]{:S(2)}) %copy-start.2) | copy-done | bytes 1048600
  5.7 0.6 shard_map.76
  6.4 16.1 %collective-permute-start = (bf16[656,512]{1,0:T(8,128)(2,1)S(1)}, bf16[656,512]{1,0:T(8,128)(2,1)S(1)}, u32[]{:S(2)}, u32[]{:S(2)}) collective-permute-start(bf16[656,512]{1,0:T(8,128)(2,1)S(1)} %get-tuple-element.12), channel_id=1, source_target_pairs={{0,32},{32,0},{64,96},{96,64},{128,160},{160,128},{192,224},{224,1... | collective-permute-start | bytes 2015240 | tf_op jit(solution)/shard_map/ppermute | solution.py:235
  22.5 1.7 %collective-permute-done.got = bf16[656,512]{1,0:T(8,128)(2,1)S(1)} collective-permute-done((bf16[656,512]{1,0:T(8,128)(2,1)S(1)}, bf16[656,512]{1,0:T(8,128)(2,1)S(1)}, u32[]{:S(2)}, u32[]{:S(2)}) %collective-permute-start) | collective-permute-done | bytes 671776 | tf_op jit(solution)/shard_map/ppermute | solution.py:235
  24.2 0.7 shard_map.77
  24.9 28.0 %all_to_all.15.got = bf16[16,208,128]{2,1,0:T(8,128)(2,1)S(1)} all-to-all(bf16[16,208,128]{2,1,0:T(8,128)(2,1)S(1)} %shard_map.77), channel_id=1, replica_groups={{0,64,128,192,256,320,384,448,512,576,640,704,768,832,896,960},{32,96,1..., dimensions={0} | all-to-all | bytes 1703936 | tf_op jit(solution)/shard_map/all_to_all | solution.py:24
  52.8 0.7 shard_map.78
  53.5 26.3 %all_to_all.16.mine = bf16[16,192,128]{2,1,0:T(8,128)(2,1)S(1)} all-to-all(bf16[16,192,128]{2,1,0:T(8,128)(2,1)S(1)} %get-tuple-element.13), channel_id=1, replica_groups={{0,64,128,192,256,320,384,448,512,576,640,704,768,832,896,960},{32,96,1..., dimensions={0} | all-to-all | bytes 1572864 | tf_op jit(solution)/shard_map/all_to_all | solution.py:24
  79.8 4.9 %collective-permute-start.1 = (bf16[16,192,128]{2,1,0:T(8,128)(2,1)S(1)}, bf16[16,192,128]{2,1,0:T(8,128)(2,1)S(1)}, u32[]{:S(2)}, u32[]{:S(2)}) collective-permute-start(bf16[16,192,128]{2,1,0:T(8,128)(2,1)S(1)} %all_to_all.16.mine), channel_id=1, source_target_pairs={{0,32},{32,0},{64,96},{96,64},{128,160},{160,128},{192,224},{224,1... | collective-permute-start | bytes 2359304 | tf_op jit(solution)/shard_map/ppermute | solution.py:246
  84.7 1.9 %collective-permute-done.1.other = bf16[16,192,128]{2,1,0:T(8,128)(2,1)S(1)} collective-permute-done((bf16[16,192,128]{2,1,0:T(8,128)(2,1)S(1)}, bf16[16,192,128]{2,1,0:T(8,128)(2,1)S(1)}, u32[]{:S(2)}, u32[]{:S(2)}) %collective-permute-start.1) | collective-permute-done | bytes 786464 | tf_op jit(solution)/shard_map/ppermute | solution.py:246
  86.6 2.7 %shard_map.79 = (bf16[1024,512]{1,0:T(8,128)(2,1)S(1)}, f32[32,8,128]{2,1,0:T(8,128)}) custom-call(s32[4]{0:T(128)S(1)} %pad_add_fusion.meta, bf16[16,192,128]{2,1,0:T(8,128)(2,1)S(1)} %all_to_all.16.mine, bf16[16,192,128]{2,1,0:T(8,128)(2,1)S(1)} %collective-permute-done.1.other, bf16[1024,512]{1,0:T(8,128)(2,1)S(1)} %copy-done.5, ...), custom_call_target="tpu_custom_call" | custom-call | flops 1073741824 | bytes 4849664 | tf_op jit(solution)/shard_map/pallas_call | solution.py:39
  89.3 12.8 %all-to-all-start.2 = ((f32[32,8,128]{2,1,0:T(8,128)}), f32[32,8,128]{2,1,0:T(8,128)S(1)}, u32[]{:S(2)}, u32[]{:S(2)}) async-start(f32[32,8,128]{2,1,0:T(8,128)} %get-tuple-element.14.squares), calls=%async_computation.2 | async-start | bytes 262144 | tf_op jit(solution)/shard_map/all_to_all | solution.py:24
  102.2 0.0 copy-start.6
  102.2 1.2 %copy-done.6 = bf16[1024,512]{1,0:T(8,128)(2,1)S(1)} copy-done((bf16[1024,512]{1,0:T(8,128)(2,1)S(1)}, bf16[1024,512]{1,0:T(8,128)(2,1)}, u32[]{:S(2)}) %copy-start.6) | copy-done | bytes 1048600
  103.4 1.1 copy-done.8
  104.5 6.0 %shard_map.81 = (bf16[1024,512]{1,0:T(8,128)(2,1)}, f32[1,1,512,512]{3,2,1,0:T(8,128)}) custom-call(s32[4]{0:T(128)S(1)} %pad_add_fusion.meta, bf16[16,192,128]{2,1,0:T(8,128)(2,1)S(1)} %all_to_all.16.mine, bf16[16,192,128]{2,1,0:T(8,128)(2,1)S(1)} %copy-done.8, f32[16,128]{1,0:T(8,128)S(1)} %get-tuple-element.16.diagonals, bf16[1024,512]{1,0:T(8,128)(2,1)S(1)} %copy-done.6, ...), custom_call_target="tpu_custom_call" | custom-call | flops 2684354560 | bytes 5906432 | tf_op jit(solution)/shard_map/pallas_call | solution.py:39
  110.6 6.7 %all-to-all-done.2.every = f32[32,8,128]{2,1,0:T(8,128)S(1)} async-done(((f32[32,8,128]{2,1,0:T(8,128)}), f32[32,8,128]{2,1,0:T(8,128)S(1)}, u32[]{:S(2)}, u32[]{:S(2)}) %all-to-all-start.2) | async-done | bytes 131104 | tf_op jit(solution)/shard_map/all_to_all | solution.py:24
  117.3 1.9 %shard_map.80 = bf16[1024,512]{1,0:T(8,128)(2,1)} custom-call(s32[4]{0:T(128)S(1)} %pad_add_fusion.meta, f32[32,8,128]{2,1,0:T(8,128)S(1)} %all-to-all-done.2.every, bf16[1024,512]{1,0:T(8,128)(2,1)S(1)} %get-tuple-element.15.rounded), custom_call_target="tpu_custom_call" | custom-call | flops 1048576 | bytes 2228224 | tf_op jit(solution)/shard_map/pallas_call | solution.py:39
  (11 shorter events, 0.0 us)
Async XLA Ops:
  0.6 0.7 copy-start
  3.3 1.2 %copy-start.1 = (bf16[1,1024,512]{2,1,0:T(8,128)(2,1)S(1)}, bf16[1,1024,512]{2,1,0:T(8,128)(2,1)}, u32[]{:S(2)}) copy-start(bf16[1,1024,512]{2,1,0:T(8,128)(2,1)} %grads.3) | copy-start | bytes 3145732
  4.5 1.2 %copy-start.2 = (f32[1,1,512,512]{3,2,1,0:T(8,128)S(1)}, f32[1,1,512,512]{3,2,1,0:T(8,128)}, u32[]{:S(2)}) copy-start(f32[1,1,512,512]{3,2,1,0:T(8,128)} %stats.3) | copy-start | bytes 3145732
  6.4 17.8 %collective-permute-start = (bf16[656,512]{1,0:T(8,128)(2,1)S(1)}, bf16[656,512]{1,0:T(8,128)(2,1)S(1)}, u32[]{:S(2)}, u32[]{:S(2)}) collective-permute-start(bf16[656,512]{1,0:T(8,128)(2,1)S(1)} %get-tuple-element.12), channel_id=1, source_target_pairs={{0,32},{32,0},{64,96},{96,64},{128,160},{160,128},{192,224},{224,1... | collective-permute-start | bytes 2015240 | tf_op jit(solution)/shard_map/ppermute | solution.py:235
  52.8 33.8 %copy-start.4 = (bf16[1024,512]{1,0:T(8,128)(2,1)S(1)}, bf16[1024,512]{1,0:T(8,128)(2,1)}, u32[]{:S(2)}) copy-start(bf16[1024,512]{1,0:T(8,128)(2,1)} %right_root.1) | copy-start | bytes 3145732
  52.8 33.8 %copy-start.5 = (bf16[1024,512]{1,0:T(8,128)(2,1)S(1)}, bf16[1024,512]{1,0:T(8,128)(2,1)}, u32[]{:S(2)}) copy-start(bf16[1024,512]{1,0:T(8,128)(2,1)} %left_root.3) | copy-start | bytes 3145732
  79.8 22.3 %copy-start.3 = (f32[1,1,512,512]{3,2,1,0:T(8,128)S(1)}, f32[1,1,512,512]{3,2,1,0:T(8,128)}, u32[]{:S(2)}) copy-start(f32[1,1,512,512]{3,2,1,0:T(8,128)} %stats.3) | copy-start | bytes 3145732
  79.8 6.8 %collective-permute-start.1 = (bf16[16,192,128]{2,1,0:T(8,128)(2,1)S(1)}, bf16[16,192,128]{2,1,0:T(8,128)(2,1)S(1)}, u32[]{:S(2)}, u32[]{:S(2)}) collective-permute-start(bf16[16,192,128]{2,1,0:T(8,128)(2,1)S(1)} %all_to_all.16.mine), channel_id=1, source_target_pairs={{0,32},{32,0},{64,96},{96,64},{128,160},{160,128},{192,224},{224,1... | collective-permute-start | bytes 2359304 | tf_op jit(solution)/shard_map/ppermute | solution.py:246
  86.6 2.7 %copy-start.7 = (bf16[16,192,128]{2,1,0:T(8,128)(2,1)}, bf16[16,192,128]{2,1,0:T(8,128)(2,1)S(1)}, u32[]{:S(2)}) copy-start(bf16[16,192,128]{2,1,0:T(8,128)(2,1)S(1)} %collective-permute-done.1.other) | copy-start | bytes 2359300
  89.3 27.9 %all-to-all-start.2 = ((f32[32,8,128]{2,1,0:T(8,128)}), f32[32,8,128]{2,1,0:T(8,128)S(1)}, u32[]{:S(2)}, u32[]{:S(2)}) async-start(f32[32,8,128]{2,1,0:T(8,128)} %get-tuple-element.14.squares), calls=%async_computation.2 | async-start | bytes 262144 | tf_op jit(solution)/shard_map/all_to_all | solution.py:24
  102.2 1.2 %copy-start.6 = (bf16[1024,512]{1,0:T(8,128)(2,1)S(1)}, bf16[1024,512]{1,0:T(8,128)(2,1)}, u32[]{:S(2)}) copy-start(bf16[1024,512]{1,0:T(8,128)(2,1)} %left_root.3) | copy-start | bytes 3145732
  103.4 1.1 copy-start.8

commit v3 on v2

v3 whole, which is shorter than its diff:
```python
import jax
import jax.numpy as jnp
from jax import lax
from jax.experimental import pallas as pl
from jax.experimental.pallas import tpu as pltpu
from jax.sharding import PartitionSpec as P

BETA = 0.95
EPSILON = 1e-06
F32 = jnp.float32
BF16 = jnp.bfloat16

WIDTH = 512
HALF = 256
TILE = 128
SLOT = 32
CHIPS = 16
N_DP = 32
FIRST = TILE + 2 * SLOT + 8
SECOND = TILE + 2 * SLOT


def exchange(array, axis, groups=None):
    return lax.all_to_all(array, axis, 0, 0, axis_index_groups=groups)


def mm(left_arg, right_arg):
    return jnp.dot(left_arg, right_arg, preferred_element_type=F32)


def row_col(rows, cols):
    shape = (rows, cols)
    return lax.broadcasted_iota(jnp.int32, shape, 0), lax.broadcasted_iota(jnp.int32, shape, 1)


def core_of():
    return lax.rem(lax.axis_index("dp"), 2)


def call(body, args, outs, flops, scratch=(), spaces=None, out_spaces=None):
    spaces = spaces or [pltpu.VMEM] * len(args)
    out_spaces = out_spaces or [pltpu.VMEM] * len(outs)
    moved = sum(a.size * a.dtype.itemsize for a in args) + sum(o.size * o.dtype.itemsize for o in outs)
    return pl.pallas_call(
        body,
        out_shape=outs,
        in_specs=[pl.BlockSpec(memory_space=space) for space in spaces],
        out_specs=[pl.BlockSpec(memory_space=space) for space in out_spaces],
        scratch_shapes=scratch,
        cost_estimate=pl.CostEstimate(flops=flops, bytes_accessed=moved, transcendentals=0),
        compiler_params=pltpu.CompilerParams(vmem_limit_bytes=16 << 20),
    )(*args)


def pack(grads, stats, send, keep, upper, lower, sems):
    core = core_of()
    other = 1 - core
    copies = [
        pltpu.make_async_copy(stats.at[0, 0, 0:TILE], upper.at[0:TILE], sems.at[0]),
        pltpu.make_async_copy(stats.at[0, 0, TILE:HALF], upper.at[TILE:HALF], sems.at[1]),
        pltpu.make_async_copy(stats.at[0, 0, HALF:, HALF:], lower, sems.at[2]),
    ]
    for part in range(2):
        for k, (block, target) in enumerate(((other, send), (core, keep))):
            source = grads.at[0, pl.ds(pl.multiple_of(block * WIDTH + part * HALF, HALF), HALF)]
            copies.append(
                pltpu.make_async_copy(source, target.at[part * HALF : part * HALF + HALF], sems.at[3 + 2 * part + k])
            )
    for copy in copies:
        copy.start()
    for copy in copies[:3]:
        copy.wait()
    row, col = row_col(HALF, HALF)
    low = lower[...]
    both = jnp.where(row <= col, upper[:, :HALF], low).astype(BF16)
    corner = upper[:, HALF:].astype(BF16)
    diagonal = jnp.sum(jnp.where(row == col, low, 0.0), axis=0, keepdims=True)
    line, _ = row_col(16, TILE)
    lines = jnp.where(line == 2 * core, diagonal[:, :TILE], jnp.where(line == 2 * core + 1, diagonal[:, TILE:], 0.0))
    lines = lines.astype(BF16)
    end = WIDTH + TILE

    @pl.when(core == 0)
    def _():
        keep[WIDTH:end, :HALF] = corner[:TILE]
        keep[WIDTH:end, HALF:] = both[:TILE]
        send[WIDTH:end, :HALF] = corner[TILE:]
        send[WIDTH:end, HALF:] = both[TILE:]

    @pl.when(core == 1)
    def _():
        keep[WIDTH:end, :HALF] = corner[TILE:]
        keep[WIDTH:end, HALF:] = both[TILE:]
        send[WIDTH:end, :HALF] = corner[:TILE]
        send[WIDTH:end, HALF:] = both[:TILE]

    for start in range(0, WIDTH, TILE):
        keep[end:, start : start + TILE] = lines
        send[end:, start : start + TILE] = lines
    for copy in copies[3:]:
        copy.wait()


def pair_add(keep, got, out):
    core = core_of()
    mine = pl.multiple_of(TILE + SLOT * core, SLOT)
    theirs = pl.multiple_of(TILE + SLOT * (1 - core), SLOT)
    lines = (keep[WIDTH + TILE :, :TILE].astype(F32) + got[WIDTH + TILE :, :TILE].astype(F32))[0:8].astype(BF16)
    for chip in range(CHIPS):
        cols = slice(TILE * (chip // 4), TILE * (chip // 4) + TILE)
        top = TILE * (chip % 4)
        own = keep[top : top + TILE, cols].astype(F32)
        out[chip, 0:TILE] = (own + got[top : top + TILE, cols].astype(F32)).astype(BF16)
        at = WIDTH + SLOT * (chip % 4)
        out[chip, pl.ds(mine, SLOT)] = keep[at : at + SLOT, cols]
        out[chip, pl.ds(theirs, SLOT)] = got[at : at + SLOT, cols]
        out[chip, SECOND:] = lines


def gather_sum(owners, got, out, diagonals):
    column = lax.axis_index("fsdp")
    total = got[0, 0:TILE].astype(F32)
    for chip in range(1, CHIPS):
        total = total + got[chip, 0:TILE].astype(F32)
    total = total.astype(BF16)
    line, _ = row_col(16, TILE)
    lines = jnp.zeros((16, TILE), F32)
    slots = []
    for i in range(2):
        owner = owners[column, i]
        chip = owner // 2
        side = owner % 2
        slots.append(got[chip, pl.ds(pl.multiple_of(TILE + SLOT * side, SLOT), SLOT)])
        rows = got[chip, SECOND:].astype(F32)
        for k in range(2):
            pick = jnp.where(side == 0, rows[k : k + 1], rows[2 + k : 3 + k])
            lines = jnp.where(line == 8 * i + k, pick, lines)
    diagonals[...] = lines
    for chip in range(CHIPS):
        out[chip, 0:TILE] = total
        for i in range(2):
            out[chip, TILE + SLOT * i : TILE + SLOT * (i + 1)] = slots[i]


def load_grad(source, grad):
    for chip in range(CHIPS):
        top = TILE * (chip % 4)
        left = TILE * (chip // 4)
        grad[top : top + TILE, left : left + TILE] = source[chip, 0:TILE]


def precondition(source, left_root, right_root, rounded, grad, block):
    rows = pl.ds(pl.multiple_of(block * WIDTH, WIDTH), WIDTH)
    load_grad(source, grad)
    product = mm(left_root[rows, :], grad[...]).astype(BF16)
    raw = mm(product, right_root[rows, :])
    rounded[...] = raw.astype(BF16)
    column = jnp.sum(raw * raw, axis=0, keepdims=True)
    return jnp.sum(column, axis=1, keepdims=True)


def own_block(mine, left_root, right_root, rounded, squares, grad):
    total = precondition(mine, left_root, right_root, rounded, grad, core_of())
    squares[...] = jnp.broadcast_to(total, squares.shape)


def other_block(other, left_root, right_root, own, rounded, squares, grad):
    total = precondition(other, left_root, right_root, rounded, grad, 1 - core_of())
    filled = own[0:1] + jnp.broadcast_to(total, (1, TILE))
    for k in range(squares.shape[0]):
        squares[k] = filled


def newton(owners, mine, other, diagonals, left_root, stats, squares, new_root, new_stats, grad, old_stats, sem):
    core = core_of()
    replica = lax.axis_index("dp")
    column = lax.axis_index("fsdp")
    fetch = pltpu.make_async_copy(stats.at[0, 0], old_stats, sem)
    fetch.start()
    owner_known = (owners[column, 0] == replica) | (owners[column, 1] == replica)
    row, col = row_col(HALF, HALF)

    @pl.when(jnp.logical_not(owner_known))
    def _():
        new_stats[...] = jnp.zeros_like(new_stats)

    fetch.wait()

    def one(block, source, first, second):
        rows = slice(block * WIDTH, (block + 1) * WIDTH)
        load_grad(source, grad)
        gram = lax.dot_general(
            grad[...], grad[...], (((1,), (1,)), ((), ())), preferred_element_type=F32
        )

        @pl.when(owners[column, block] == replica)
        def _():
            new_stats[0, 0] = BETA * old_stats[...] + (1.0 - BETA) * gram

        start = TILE + SLOT * block

        def panel(part, k):
            return part[4 * k : 4 * k + 4, start : start + SLOT].reshape(TILE, TILE)

        packed = [
            jnp.concatenate(
                [jnp.concatenate([panel(part, k), panel(part, k + 1)], axis=1) for part in (first, second)], axis=0
            ).astype(F32)
            for k in (0, 2)
        ]
        corner, both = packed
        corner_t = jnp.transpose(corner)
        both_t = jnp.transpose(both)
        diagonal = jnp.concatenate(
            [diagonals[8 * block : 8 * block + 1], diagonals[8 * block + 1 : 8 * block + 2]], axis=1
        )
        high = jnp.where(row <= col, both, both_t)
        low = jnp.where(row > col, both, jnp.where(row == col, diagonal, both_t))
        old = jnp.concatenate(
            [jnp.concatenate([high, corner], axis=1), jnp.concatenate([corner_t, low], axis=1)], axis=0
        )
        fresh = (BETA * old + (1.0 - BETA) * gram).astype(BF16)
        left = left_root[rows, :]
        square = mm(left, left).astype(BF16)
        cube = mm(left, square).astype(BF16)
        change = mm(cube, mm(fresh, square).astype(BF16))
        new_root[rows, :] = (1.25 * left.astype(F32) - 0.25 * change).astype(BF16)

    @pl.when(core == 0)
    def _():
        one(0, mine, mine, other)
        one(1, other, mine, other)

    @pl.when(core == 1)
    def _():
        one(0, other, other, mine)
        one(1, mine, other, mine)


def rescale(count):
    def body(every, own, other, update, buffer, sems):
        core = core_of()
        total = every[0]
        for k in range(1, every.shape[0]):
            total = total + every[k]
        scale = lax.rsqrt(total[:, 0:1] / count + EPSILON)
        copies = []
        for source, block in ((own, core), (other, 1 - core)):
            for start in range(0, WIDTH, TILE):
                k = len(copies)
                buffer[k] = (source[start : start + TILE].astype(F32) * scale).astype(BF16)
                to = update.at[pl.ds(pl.multiple_of(block * WIDTH + start, TILE), TILE)]
                copies.append(pltpu.make_async_copy(buffer.at[k], to, sems.at[k]))
                copies[-1].start()
        for copy in copies:
            copy.wait()

    return body


def local(grads, stats, left_root, right_root, owners):
    n_fsdp = lax.axis_size("fsdp")
    rows = left_root.shape[0]
    same_core = [[2 * k + core for k in range(CHIPS)] for core in range(2)]
    swap = [(k, k ^ 1) for k in range(N_DP)]
    shape = jax.ShapeDtypeStruct
    product = 2 * WIDTH**3
    vmem = pltpu.VMEM
    grads, stats = [pltpu.with_memory_space_constraint(array, pltpu.HBM) for array in (grads, stats)]
    block = vmem((WIDTH, WIDTH), BF16)
    packed = WIDTH + TILE + 16

    send, keep = call(
        pack,
        [grads, stats],
        [shape((packed, WIDTH), BF16), shape((packed, WIDTH), BF16)],
        1 << 20,
        [vmem((HALF, WIDTH), F32), vmem((HALF, HALF), F32), pltpu.SemaphoreType.DMA((7,))],
        [pltpu.HBM, pltpu.HBM],
    )
    got = lax.ppermute(send, "dp", swap)
    (payload,) = call(pair_add, [keep, got], [shape((CHIPS, FIRST, TILE), BF16)], 1 << 20)
    arrived = exchange(payload, "dp", same_core)
    repeated, diagonals = call(
        gather_sum,
        [owners, arrived],
        [shape((CHIPS, SECOND, TILE), BF16), shape((16, TILE), F32)],
        1 << 20,
        spaces=[pltpu.SMEM, vmem],
    )
    mine = exchange(repeated, "dp", same_core)
    other = lax.ppermute(mine, "dp", swap)
    own_rounded, own_squares = call(
        own_block,
        [mine, left_root, right_root],
        [shape((WIDTH, WIDTH), BF16), shape((8, TILE), F32)],
        2 * product,
        [block],
    )
    other_rounded, squares = call(
        other_block,
        [other, left_root, right_root, own_squares],
        [shape((WIDTH, WIDTH), BF16), shape((n_fsdp, 1, TILE), F32)],
        2 * product,
        [block],
    )
    every = exchange(squares, "fsdp")
    new_root, new_stats = call(
        newton,
        [owners, mine, other, diagonals, left_root, stats, squares],
        [shape((rows, WIDTH), BF16), shape((1, 1, WIDTH, WIDTH), F32)],
        10 * product,
        [block, vmem((WIDTH, WIDTH), F32), pltpu.SemaphoreType.DMA],
        [pltpu.SMEM, vmem, vmem, vmem, vmem, pltpu.HBM, vmem],
    )
    (update,) = call(
        rescale(float(rows * WIDTH * n_fsdp)),
        [every, own_rounded, other_rounded],
        [shape((rows, WIDTH), BF16)],
        1 << 20,
        [vmem((8, TILE, WIDTH), BF16), pltpu.SemaphoreType.DMA((8,))],
        out_spaces=[pltpu.HBM],
    )
    return (update, new_stats, new_root)


def solution(mesh):
    in_specs = (
        P("dp", None, "fsdp"),
        P("dp", "fsdp", None, None),
        P(None, "fsdp"),
        P(None, "fsdp"),
        P(),
    )
    out_specs = (P(None, "fsdp"), P("dp", "fsdp", None, None), P(None, "fsdp"))
    return jax.shard_map(local, mesh=mesh, in_specs=in_specs, out_specs=out_specs, check_vma=False)
```

time: 120 us -> 111 us (0.925)
  blocking collectives: 54.3 us -> 28.3 us
  waiting for transfers between devices: 10.3 us -> 29.7 us
  local copies, waits for them, and re-layouts: 6.08 us -> 2.03 us
  starting transfers between devices: 33.8 us -> 36.3 us
  Pallas kernels: 12.6 us -> 14 us
  other arithmetic: 1.37 us -> 0 us
    all_to_all x2 -> x1, blocking collectives: 54.3 us -> 28.3 us  [exchange(): return lax.all_to_all(array, axis, 0, 0, axis_index_groups=groups)]
    all_to_all x1 -> x2, waiting for transfers between devices: 6.7 us -> 26.9 us  [exchange(): return lax.all_to_all(array, axis, 0, 0, axis_index_groups=groups)]
    unnamed x18 -> x15, local copies, waits for them, and re-layouts: 5.49 us -> 2.03 us
    all_to_all x1 -> x2, starting transfers between devices: 12.8 us -> 15.8 us  [exchange(): return lax.all_to_all(array, axis, 0, 0, axis_index_groups=groups)]
    pallas_call x6 -> x7, Pallas kernels: 12.6 us -> 14 us  [call(): pl.pallas_call(body, out_shape=outs, in_specs=[pl.BlockSpec(memory_space=...]
    another operation x1 -> x0, other arithmetic: 1.37 us -> none  [local(): jnp.stack([lax.rem(replica, 2), owner_row[0], owner_row[1], replica])]
  transfers between devices with their start and end apart: 3 -> 4, of which waited for: 3 -> 4; matrix products, arithmetic and copies ran while one was open for 0% -> 0% of each run, Pallas kernels for 5% -> 7%
where the time goes in v3:
time: 111 us
  starting transfers between devices  36.3 us (33%)
  waiting for transfers between devices  29.7 us (27%)
  blocking collectives  28.3 us (25%)
  Pallas kernels  14 us (13%)
  local copies, waits for them, and re-layouts  2.03 us (2%)
    all_to_all x1, blocking collectives, exchange(): return lax.all_to_all(array, axis, 0, 0, axis_index_groups=groups)  28.3 us
    all_to_all x2, waiting for transfers between devices, exchange(): return lax.all_to_all(array, axis, 0, 0, axis_index_groups=groups)  26.9 us
    ppermute x1, starting transfers between devices, local(): got = lax.ppermute(send, 'dp', swap)  16.1 us
    all_to_all x2, starting transfers between devices, exchange(): return lax.all_to_all(array, axis, 0, 0, axis_index_groups=groups)  15.8 us
    pallas_call x7, Pallas kernels, call(): pl.pallas_call(body, out_shape=outs, in_specs=[pl.BlockSpec(memory_space=...  14 us
    ppermute x1, starting transfers between devices, local(): other = lax.ppermute(mine, 'dp', swap)  4.41 us
  transfers between devices with their start and end apart: 4, of which 4 were waited for; matrix products, arithmetic and copies ran while one was open for 0% of the time, Pallas kernels for 7%

profile of v3, /device:TPU:1, one launch (start us, length us, event | category | flops | bytes accessed | tf_op | source)
XLA Modules:
  0.0 111.0 jit_solution(9436436914794932919)
XLA Ops:
  0.6 1.5 %shard_map.76 = (bf16[656,512]{1,0:T(8,128)(2,1)S(1)}, bf16[656,512]{1,0:T(8,128)(2,1)S(1)}) custom-call(bf16[1,1024,512]{2,1,0:T(8,128)(2,1)} %grads.1, f32[1,1,512,512]{3,2,1,0:T(8,128)} %stats.3), custom_call_target="tpu_custom_call" | custom-call | flops 1048576 | bytes 3440640 | tf_op jit(solution)/shard_map/pallas_call | solution.py:44
  2.1 16.1 %collective-permute-start = (bf16[656,512]{1,0:T(8,128)(2,1)S(1)}, bf16[656,512]{1,0:T(8,128)(2,1)S(1)}, u32[]{:S(2)}, u32[]{:S(2)}) collective-permute-start(bf16[656,512]{1,0:T(8,128)(2,1)S(1)} %get-tuple-element.14), channel_id=1, source_target_pairs={{0,32},{32,0},{64,96},{96,64},{128,160},{160,128},{192,224},{224,1... | collective-permute-start | bytes 2015240 | tf_op jit(solution)/shard_map/ppermute | solution.py:281
  18.2 1.7 %collective-permute-done.got = bf16[656,512]{1,0:T(8,128)(2,1)S(1)} collective-permute-done((bf16[656,512]{1,0:T(8,128)(2,1)S(1)}, bf16[656,512]{1,0:T(8,128)(2,1)S(1)}, u32[]{:S(2)}, u32[]{:S(2)}) %collective-permute-start) | collective-permute-done | bytes 671776 | tf_op jit(solution)/shard_map/ppermute | solution.py:281
  19.9 1.0 shard_map.77
  21.0 3.8 %all-to-all-start = ((bf16[16,200,128]{2,1,0:T(8,128)(2,1)}), bf16[16,200,128]{2,1,0:T(8,128)(2,1)S(1)}, u32[]{:S(2)}, u32[]{:S(2)}) async-start(bf16[16,200,128]{2,1,0:T(8,128)(2,1)} %shard_map.77), calls=%async_computation | async-start | bytes 1638400 | tf_op jit(solution)/shard_map/all_to_all | solution.py:24
  24.7 0.0 copy-done.6
  24.7 0.1 copy.8.owners
  24.8 22.9 %all-to-all-done.got = bf16[16,200,128]{2,1,0:T(8,128)(2,1)S(1)} async-done(((bf16[16,200,128]{2,1,0:T(8,128)(2,1)}), bf16[16,200,128]{2,1,0:T(8,128)(2,1)S(1)}, u32[]{:S(2)}, u32[]{:S(2)}) %all-to-all-start) | async-done | bytes 819232 | tf_op jit(solution)/shard_map/all_to_all | solution.py:24
  47.7 0.9 shard_map.78
  48.7 28.3 %all_to_all.15.mine = bf16[16,192,128]{2,1,0:T(8,128)(2,1)S(1)} all-to-all(bf16[16,192,128]{2,1,0:T(8,128)(2,1)S(1)} %get-tuple-element.15), channel_id=1, replica_groups={{0,64,128,192,256,320,384,448,512,576,640,704,768,832,896,960},{32,96,1..., dimensions={0} | all-to-all | bytes 1572864 | tf_op jit(solution)/shard_map/all_to_all | solution.py:24
  77.0 4.4 %collective-permute-start.1 = (bf16[16,192,128]{2,1,0:T(8,128)(2,1)S(1)}, bf16[16,192,128]{2,1,0:T(8,128)(2,1)S(1)}, u32[]{:S(2)}, u32[]{:S(2)}) collective-permute-start(bf16[16,192,128]{2,1,0:T(8,128)(2,1)S(1)} %all_to_all.15.mine), channel_id=1, source_target_pairs={{0,32},{32,0},{64,96},{96,64},{128,160},{160,128},{192,224},{224,1... | collective-permute-start | bytes 2359304 | tf_op jit(solution)/shard_map/ppermute | solution.py:292
  81.4 0.0 copy-done
  81.4 0.0 copy-done.1
  81.4 0.8 shard_map.79
  82.2 1.0 collective-permute-done.1.other
  83.3 1.5 %shard_map.80 = (bf16[512,512]{1,0:T(8,128)(2,1)S(1)}, f32[32,1,128]{2,1,0:T(1,128)}) custom-call(bf16[16,192,128]{2,1,0:T(8,128)(2,1)S(1)} %collective-permute-done.1.other, bf16[1024,512]{1,0:T(8,128)(2,1)S(1)} %copy-done.1, bf16[1024,512]{1,0:T(8,128)(2,1)S(1)} %copy-done, f32[8,128]{1,0:T(8,128)S(1)} %get-tuple-element.16.own), custom_call_target="tpu_custom_call" | custom-call | flops 536870912 | bytes 3428352 | tf_op jit(solution)/shard_map/pallas_call | solution.py:44
  84.7 0.0 copy-done.2
  84.7 0.8 copy-done.4
  85.5 12.1 %all-to-all-start.2 = ((f32[32,1,128]{2,1,0:T(1,128)}), f32[32,1,128]{2,1,0:T(1,128)S(1)}, u32[]{:S(2)}, u32[]{:S(2)}) async-start(f32[32,1,128]{2,1,0:T(1,128)} %get-tuple-element.17.squares), calls=%async_computation.2 | async-start | bytes 32768 | tf_op jit(solution)/shard_map/all_to_all | solution.py:24
  97.6 0.0 copy-start.3
  97.6 1.1 %copy-done.3 = bf16[16,192,128]{2,1,0:T(8,128)(2,1)S(1)} copy-done((bf16[16,192,128]{2,1,0:T(8,128)(2,1)S(1)}, bf16[16,192,128]{2,1,0:T(8,128)(2,1)}, u32[]{:S(2)}) %copy-start.3) | copy-done | bytes 786456
  98.7 7.0 %shard_map.82 = (bf16[1024,512]{1,0:T(8,128)(2,1)}, f32[1,1,512,512]{3,2,1,0:T(8,128)}) custom-call(s32[32,2]{1,0:T(8,128)S(1)} %copy.8.owners, bf16[16,192,128]{2,1,0:T(8,128)(2,1)S(1)} %all_to_all.15.mine, bf16[16,192,128]{2,1,0:T(8,128)(2,1)S(1)} %copy-done.3, f32[16,128]{1,0:T(8,128)S(1)} %get-tuple-element.20.diagonals, ...), custom_call_target="tpu_custom_call" | custom-call | flops 2684354560 | bytes 5792000 | tf_op jit(solution)/shard_map/pallas_call | solution.py:44
  105.8 4.0 %all-to-all-done.2.every = f32[32,1,128]{2,1,0:T(1,128)S(1)} async-done(((f32[32,1,128]{2,1,0:T(1,128)}), f32[32,1,128]{2,1,0:T(1,128)S(1)}, u32[]{:S(2)}, u32[]{:S(2)}) %all-to-all-start.2) | async-done | bytes 16416 | tf_op jit(solution)/shard_map/all_to_all | solution.py:24
  109.8 1.2 %shard_map.81 = bf16[1024,512]{1,0:T(8,128)(2,1)} custom-call(f32[32,1,128]{2,1,0:T(1,128)S(1)} %all-to-all-done.2.every, bf16[512,512]{1,0:T(8,128)(2,1)S(1)} %get-tuple-element.18.own, bf16[512,512]{1,0:T(8,128)(2,1)S(1)} %copy-done.5), custom_call_target="tpu_custom_call" | custom-call | flops 1048576 | bytes 2113536 | tf_op jit(solution)/shard_map/pallas_call | solution.py:44
  (7 shorter events, 0.0 us)
Async XLA Ops:
  2.1 17.8 %collective-permute-start = (bf16[656,512]{1,0:T(8,128)(2,1)S(1)}, bf16[656,512]{1,0:T(8,128)(2,1)S(1)}, u32[]{:S(2)}, u32[]{:S(2)}) collective-permute-start(bf16[656,512]{1,0:T(8,128)(2,1)S(1)} %get-tuple-element.14), channel_id=1, source_target_pairs={{0,32},{32,0},{64,96},{96,64},{128,160},{160,128},{192,224},{224,1... | collective-permute-start | bytes 2015240 | tf_op jit(solution)/shard_map/ppermute | solution.py:281
  21.0 3.8 %copy-start.6 = (s32[32,2]{0,1:T(2,128)S(1)}, s32[32,2]{0,1:T(2,128)}, u32[]{:S(2)}) copy-start(s32[32,2]{0,1:T(2,128)} %param.9) | copy-start | bytes 772
  21.0 26.8 %all-to-all-start = ((bf16[16,200,128]{2,1,0:T(8,128)(2,1)}), bf16[16,200,128]{2,1,0:T(8,128)(2,1)S(1)}, u32[]{:S(2)}, u32[]{:S(2)}) async-start(bf16[16,200,128]{2,1,0:T(8,128)(2,1)} %shard_map.77), calls=%async_computation | async-start | bytes 1638400 | tf_op jit(solution)/shard_map/all_to_all | solution.py:24
  24.8 56.5 %copy-start = (bf16[1024,512]{1,0:T(8,128)(2,1)S(1)}, bf16[1024,512]{1,0:T(8,128)(2,1)}, u32[]{:S(2)}) copy-start(bf16[1024,512]{1,0:T(8,128)(2,1)} %right_root.3) | copy-start | bytes 3145732
  24.8 56.6 %copy-start.1 = (bf16[1024,512]{1,0:T(8,128)(2,1)S(1)}, bf16[1024,512]{1,0:T(8,128)(2,1)}, u32[]{:S(2)}) copy-start(bf16[1024,512]{1,0:T(8,128)(2,1)} %left_root.5) | copy-start | bytes 3145732
  77.0 6.3 %collective-permute-start.1 = (bf16[16,192,128]{2,1,0:T(8,128)(2,1)S(1)}, bf16[16,192,128]{2,1,0:T(8,128)(2,1)S(1)}, u32[]{:S(2)}, u32[]{:S(2)}) collective-permute-start(bf16[16,192,128]{2,1,0:T(8,128)(2,1)S(1)} %all_to_all.15.mine), channel_id=1, source_target_pairs={{0,32},{32,0},{64,96},{96,64},{128,160},{160,128},{192,224},{224,1... | collective-permute-start | bytes 2359304 | tf_op jit(solution)/shard_map/ppermute | solution.py:292
  83.3 1.5 %copy-start.2 = (bf16[16,192,128]{2,1,0:T(8,128)(2,1)}, bf16[16,192,128]{2,1,0:T(8,128)(2,1)S(1)}, u32[]{:S(2)}) copy-start(bf16[16,192,128]{2,1,0:T(8,128)(2,1)S(1)} %collective-permute-done.1.other) | copy-start | bytes 2359300
  84.7 0.8 copy-start.4
  85.5 24.3 %all-to-all-start.2 = ((f32[32,1,128]{2,1,0:T(1,128)}), f32[32,1,128]{2,1,0:T(1,128)S(1)}, u32[]{:S(2)}, u32[]{:S(2)}) async-start(f32[32,1,128]{2,1,0:T(1,128)} %get-tuple-element.17.squares), calls=%async_computation.2 | async-start | bytes 32768 | tf_op jit(solution)/shard_map/all_to_all | solution.py:24
  97.6 1.1 %copy-start.3 = (bf16[16,192,128]{2,1,0:T(8,128)(2,1)S(1)}, bf16[16,192,128]{2,1,0:T(8,128)(2,1)}, u32[]{:S(2)}) copy-start(bf16[16,192,128]{2,1,0:T(8,128)(2,1)} %copy-done.2) | copy-start | bytes 2359300
  98.7 11.1 %copy-start.5 = (bf16[512,512]{1,0:T(8,128)(2,1)S(1)}, bf16[512,512]{1,0:T(8,128)(2,1)}, u32[]{:S(2)}) copy-start(bf16[512,512]{1,0:T(8,128)(2,1)} %copy-done.4) | copy-start | bytes 1572868

commit v4 on v3

--- a/solution.py
+++ b/solution.py
@@ -149,34 +149,54 @@
         grad[top : top + TILE, left : left + TILE] = source[chip, 0:TILE]
 
 
-def precondition(source, left_root, right_root, rounded, grad, block):
-    rows = pl.ds(pl.multiple_of(block * WIDTH, WIDTH), WIDTH)
-    load_grad(source, grad)
-    product = mm(left_root[rows, :], grad[...]).astype(BF16)
-    raw = mm(product, right_root[rows, :])
+def precondition(grad, left, right):
+    return mm(mm(left, grad).astype(BF16), right)
+
+
+def own_block(mine, left_root, right_root, rounded, squares, grad):
+    rows = pl.ds(pl.multiple_of(core_of() * WIDTH, WIDTH), WIDTH)
+    load_grad(mine, grad)
+    raw = precondition(grad[...], left_root[rows, :], right_root[rows, :])
     rounded[...] = raw.astype(BF16)
     column = jnp.sum(raw * raw, axis=0, keepdims=True)
-    return jnp.sum(column, axis=1, keepdims=True)
-
-
-def own_block(mine, left_root, right_root, rounded, squares, grad):
-    total = precondition(mine, left_root, right_root, rounded, grad, core_of())
-    squares[...] = jnp.broadcast_to(total, squares.shape)
-
-
-def other_block(other, left_root, right_root, own, rounded, squares, grad):
-    total = precondition(other, left_root, right_root, rounded, grad, 1 - core_of())
-    filled = own[0:1] + jnp.broadcast_to(total, (1, TILE))
+    filled = jnp.broadcast_to(jnp.sum(column, axis=1, keepdims=True), (1, TILE))
     for k in range(squares.shape[0]):
         squares[k] = filled
 
 
-def newton(owners, mine, other, diagonals, left_root, stats, squares, new_root, new_stats, grad, old_stats, sem):
+def powers(left_root, square, cube, square_buffer, cube_buffer, sems):
+    copies = []
+    for block in range(2):
+        rows = slice(block * WIDTH, (block + 1) * WIDTH)
+        left = left_root[rows, :]
+        second = mm(left, left).astype(BF16)
+        square_buffer[rows, :] = second
+        cube_buffer[rows, :] = mm(left, second).astype(BF16)
+        for k, (source, target) in enumerate(((square_buffer, square), (cube_buffer, cube))):
+            copies.append(pltpu.make_async_copy(source.at[rows], target.at[rows], sems.at[2 * block + k]))
+            copies[-1].start()
+    for copy in copies:
+        copy.wait()
+
+
+def late(
+    owners, mine, other, diagonals, left_hbm, right_hbm, square_hbm, cube_hbm, stats,
+    rounded, new_root, new_stats,
+    grad, left_root, right_part, square, cube, old_stats, sems,
+):
     core = core_of()
     replica = lax.axis_index("dp")
     column = lax.axis_index("fsdp")
-    fetch = pltpu.make_async_copy(stats.at[0, 0], old_stats, sem)
-    fetch.start()
+    rest = pl.ds(pl.multiple_of((1 - core) * WIDTH, WIDTH), WIDTH)
+    copies = [
+        pltpu.make_async_copy(left_hbm, left_root, sems.at[0]),
+        pltpu.make_async_copy(right_hbm.at[rest], right_part, sems.at[1]),
+        pltpu.make_async_copy(square_hbm, square, sems.at[2]),
+        pltpu.make_async_copy(cube_hbm, cube, sems.at[3]),
+        pltpu.make_async_copy(stats.at[0, 0], old_stats, sems.at[4]),
+    ]
+    for copy in copies:
+        copy.start()
     owner_known = (owners[column, 0] == replica) | (owners[column, 1] == replica)
     row, col = row_col(HALF, HALF)
 
@@ -184,11 +204,17 @@
     def _():
         new_stats[...] = jnp.zeros_like(new_stats)
 
-    fetch.wait()
-
-    def one(block, source, first, second):
+    for copy in copies[:2]:
+        copy.wait()
+    load_grad(other, grad)
+    rounded[...] = precondition(grad[...], left_root[rest, :], right_part[...]).astype(BF16)
+    for copy in copies[2:]:
+        copy.wait()
+
+    def one(block, source, first, second, loaded):
         rows = slice(block * WIDTH, (block + 1) * WIDTH)
-        load_grad(source, grad)
+        if not loaded:
+            load_grad(source, grad)
         gram = lax.dot_general(
             grad[...], grad[...], (((1,), (1,)), ((), ())), preferred_element_type=F32
         )
@@ -220,29 +246,30 @@
             [jnp.concatenate([high, corner], axis=1), jnp.concatenate([corner_t, low], axis=1)], axis=0
         )
         fresh = (BETA * old + (1.0 - BETA) * gram).astype(BF16)
-        left = left_root[rows, :]
-        square = mm(left, left).astype(BF16)
-        cube = mm(left, square).astype(BF16)
-        change = mm(cube, mm(fresh, square).astype(BF16))
-        new_root[rows, :] = (1.25 * left.astype(F32) - 0.25 * change).astype(BF16)
+        change = mm(cube[rows, :], mm(fresh, square[rows, :]).astype(BF16))
+        new_root[rows, :] = (1.25 * left_root[rows, :].astype(F32) - 0.25 * change).astype(BF16)
 
     @pl.when(core == 0)
     def _():
-        one(0, mine, mine, other)
-        one(1, other, mine, other)
+        one(1, other, mine, other, True)
+        one(0, mine, mine, other, False)
 
     @pl.when(core == 1)
     def _():
-        one(0, other, other, mine)
-        one(1, mine, other, mine)
+        one(0, other, other, mine, True)
+        one(1, mine, other, mine, False)
 
 
 def rescale(count):
-    def body(every, own, other, update, buffer, sems):
+    def body(own_every, other_every, own, other, update, buffer, sems):
         core = core_of()
-        total = every[0]
-        for k in range(1, every.shape[0]):
-            total = total + every[k]
+        totals = []
+        for every in (own_every, other_every):
+            total = every[0]
+            for k in range(1, every.shape[0]):
+                total = total + every[k]
+            totals.append(total)
+        total = totals[0] + totals[1]
         scale = lax.rsqrt(total[:, 0:1] / count + EPSILON)
         copies = []
         for source, block in ((own, core), (other, 1 - core)):
@@ -281,6 +308,16 @@
     got = lax.ppermute(send, "dp", swap)
     (payload,) = call(pair_add, [keep, got], [shape((CHIPS, FIRST, TILE), BF16)], 1 << 20)
     arrived = exchange(payload, "dp", same_core)
+    whole = shape((rows, WIDTH), BF16)
+    square, cube = call(
+        powers,
+        [left_root],
+        [whole, whole],
+        4 * product,
+        [vmem((rows, WIDTH), BF16), vmem((rows, WIDTH), BF16), pltpu.SemaphoreType.DMA((4,))],
+        out_spaces=[pltpu.HBM, pltpu.HBM],
+    )
+    arrived, square, cube = lax.optimization_barrier((arrived, square, cube))
     repeated, diagonals = call(
         gather_sum,
         [owners, arrived],
@@ -289,33 +326,40 @@
         spaces=[pltpu.SMEM, vmem],
     )
     mine = exchange(repeated, "dp", same_core)
-    other = lax.ppermute(mine, "dp", swap)
-    own_rounded, own_squares = call(
+    own_rounded, squares = call(
         own_block,
         [mine, left_root, right_root],
-        [shape((WIDTH, WIDTH), BF16), shape((8, TILE), F32)],
-        2 * product,
-        [block],
-    )
-    other_rounded, squares = call(
-        other_block,
-        [other, left_root, right_root, own_squares],
         [shape((WIDTH, WIDTH), BF16), shape((n_fsdp, 1, TILE), F32)],
         2 * product,
         [block],
     )
-    every = exchange(squares, "fsdp")
-    new_root, new_stats = call(
-        newton,
-        [owners, mine, other, diagonals, left_root, stats, squares],
-        [shape((rows, WIDTH), BF16), shape((1, 1, WIDTH, WIDTH), F32)],
-        10 * product,
-        [block, vmem((WIDTH, WIDTH), F32), pltpu.SemaphoreType.DMA],
-        [pltpu.SMEM, vmem, vmem, vmem, vmem, pltpu.HBM, vmem],
-    )
+    own_every = exchange(squares, "fsdp")
+    after, _ = lax.optimization_barrier((mine, squares))
+    other = lax.ppermute(after, "dp", swap)
+    left_hbm, right_hbm, square, cube = [
+        pltpu.with_memory_space_constraint(array, pltpu.HBM) for array in (left_root, right_root, square, cube)
+    ]
+    other_rounded, new_root, new_stats = call(
+        late,
+        [owners, mine, other, diagonals, left_hbm, right_hbm, square, cube, stats],
+        [shape((WIDTH, WIDTH), BF16), whole, shape((1, 1, WIDTH, WIDTH), F32)],
+        8 * product,
+        [
+            block,
+            vmem((rows, WIDTH), BF16),
+            block,
+            vmem((rows, WIDTH), BF16),
+            vmem((rows, WIDTH), BF16),
+            vmem((WIDTH, WIDTH), F32),
+            pltpu.SemaphoreType.DMA((5,)),
+        ],
+        [pltpu.SMEM, vmem, vmem, vmem] + [pltpu.HBM] * 5,
+    )
+    own_every, other_rounded, new_root = lax.optimization_barrier((own_every, other_rounded, new_root))
+    other_every = lax.ppermute(own_every, "dp", swap)
     (update,) = call(
         rescale(float(rows * WIDTH * n_fsdp)),
-        [every, own_rounded, other_rounded],
+        [own_every, other_every, own_rounded, other_rounded],
         [shape((rows, WIDTH), BF16)],
         1 << 20,
         [vmem((8, TILE, WIDTH), BF16), pltpu.SemaphoreType.DMA((8,))],

time: 111 us -> 113 us (1.018)
  starting transfers between devices: 36.3 us -> 39.6 us
  waiting for transfers between devices: 29.7 us -> 26.9 us
    ppermute x1 -> x2, starting transfers between devices: 4.41 us -> 7.68 us  [the longest x1 4.41 us: local(): other = lax.ppermute(after, 'dp', swap)]
    all_to_all x2, waiting for transfers between devices: 26.9 us -> 24.3 us  [exchange(): return lax.all_to_all(array, axis, 0, 0, axis_index_groups=groups)]
  transfers between devices with their start and end apart: 4 -> 5, of which waited for: 4 -> 4; matrix products, arithmetic and copies ran while one was open for 0% -> 0% of each run, Pallas kernels for 7% -> 8%
where the time goes in v4:
time: 113 us; the launch traced here: 112 us
  starting transfers between devices  39.6 us (35%)
  blocking collectives  28.3 us (25%)
  waiting for transfers between devices  26.9 us (24%)
  Pallas kernels  14.9 us (13%)
  local copies, waits for them, and re-layouts  2.04 us (2%)
    all_to_all x1, blocking collectives, exchange(): return lax.all_to_all(array, axis, 0, 0, axis_index_groups=groups)  28.3 us
    all_to_all x2, waiting for transfers between devices, exchange(): return lax.all_to_all(array, axis, 0, 0, axis_index_groups=groups)  24.3 us
    ppermute x1, starting transfers between devices, local(): got = lax.ppermute(send, 'dp', swap)  16.1 us
    all_to_all x2, starting transfers between devices, exchange(): return lax.all_to_all(array, axis, 0, 0, axis_index_groups=groups)  15.8 us
    pallas_call x7, Pallas kernels, call(): pl.pallas_call(body, out_shape=outs, in_specs=[pl.BlockSpec(memory_space=...  14.9 us
    ppermute x1, starting transfers between devices, local(): other = lax.ppermute(after, 'dp', swap)  4.41 us
    ppermute x1, starting transfers between devices, local(): other_every = lax.ppermute(own_every, 'dp', swap)  3.28 us
  transfers between devices with their start and end apart: 5, of which 4 were waited for; matrix products, arithmetic and copies ran while one was open for 0% of the time, Pallas kernels for 8%

profile of v4, /device:TPU:1, one launch (start us, length us, event | category | flops | bytes accessed | tf_op | source)
XLA Modules:
  0.0 112.4 jit_solution(6330230750970010046)
XLA Ops:
  0.6 1.5 %shard_map.76 = (bf16[656,512]{1,0:T(8,128)(2,1)S(1)}, bf16[656,512]{1,0:T(8,128)(2,1)S(1)}) custom-call(bf16[1,1024,512]{2,1,0:T(8,128)(2,1)} %grads.1, f32[1,1,512,512]{3,2,1,0:T(8,128)} %stats.3), custom_call_target="tpu_custom_call" | custom-call | flops 1048576 | bytes 3440640 | tf_op jit(solution)/shard_map/pallas_call | solution.py:44
  2.1 16.1 %collective-permute-start = (bf16[656,512]{1,0:T(8,128)(2,1)S(1)}, bf16[656,512]{1,0:T(8,128)(2,1)S(1)}, u32[]{:S(2)}, u32[]{:S(2)}) collective-permute-start(bf16[656,512]{1,0:T(8,128)(2,1)S(1)} %get-tuple-element.22), channel_id=1, source_target_pairs={{0,32},{32,0},{64,96},{96,64},{128,160},{160,128},{192,224},{224,1... | collective-permute-start | bytes 2015240 | tf_op jit(solution)/shard_map/ppermute | solution.py:308
  18.2 1.7 %collective-permute-done.got = bf16[656,512]{1,0:T(8,128)(2,1)S(1)} collective-permute-done((bf16[656,512]{1,0:T(8,128)(2,1)S(1)}, bf16[656,512]{1,0:T(8,128)(2,1)S(1)}, u32[]{:S(2)}, u32[]{:S(2)}) %collective-permute-start) | collective-permute-done | bytes 671776 | tf_op jit(solution)/shard_map/ppermute | solution.py:308
  19.9 1.0 shard_map.77
  21.0 3.8 %all-to-all-start = ((bf16[16,200,128]{2,1,0:T(8,128)(2,1)}), bf16[16,200,128]{2,1,0:T(8,128)(2,1)S(1)}, u32[]{:S(2)}, u32[]{:S(2)}) async-start(bf16[16,200,128]{2,1,0:T(8,128)(2,1)} %shard_map.77), calls=%async_computation | async-start | bytes 1638400 | tf_op jit(solution)/shard_map/all_to_all | solution.py:24
  24.7 0.0 copy-done.4
  24.7 0.1 copy.8.owners
  24.8 0.0 copy-done
  24.8 1.8 %shard_map.78 = (bf16[1024,512]{1,0:T(8,128)(2,1)S(1)}, bf16[1024,512]{1,0:T(8,128)(2,1)S(1)}) custom-call(bf16[1024,512]{1,0:T(8,128)(2,1)S(1)} %copy-done), custom_call_target="tpu_custom_call" | custom-call | flops 1073741824 | bytes 3145728 | tf_op jit(solution)/shard_map/pallas_call | solution.py:44
  26.6 0.0 copy-start.2
  26.6 1.0 copy-done.2
  27.6 1.0 copy-done.3
  28.5 19.2 %all-to-all-done.got = bf16[16,200,128]{2,1,0:T(8,128)(2,1)S(1)} async-done(((bf16[16,200,128]{2,1,0:T(8,128)(2,1)}), bf16[16,200,128]{2,1,0:T(8,128)(2,1)S(1)}, u32[]{:S(2)}, u32[]{:S(2)}) %all-to-all-start) | async-done | bytes 819232 | tf_op jit(solution)/shard_map/all_to_all | solution.py:24
  47.7 0.9 shard_map.79
  48.7 28.3 %all_to_all.15.mine = bf16[16,192,128]{2,1,0:T(8,128)(2,1)S(1)} all-to-all(bf16[16,192,128]{2,1,0:T(8,128)(2,1)S(1)} %get-tuple-element.26), channel_id=1, replica_groups={{0,64,128,192,256,320,384,448,512,576,640,704,768,832,896,960},{32,96,1..., dimensions={0} | all-to-all | bytes 1572864 | tf_op jit(solution)/shard_map/all_to_all | solution.py:24
  77.0 1.5 %shard_map.80 = (bf16[512,512]{1,0:T(8,128)(2,1)S(1)}, f32[32,1,128]{2,1,0:T(1,128)}) custom-call(bf16[16,192,128]{2,1,0:T(8,128)(2,1)S(1)} %all_to_all.15.mine, bf16[1024,512]{1,0:T(8,128)(2,1)S(1)} %copy-done, bf16[1024,512]{1,0:T(8,128)(2,1)S(1)} %copy-done.1), custom_call_target="tpu_custom_call" | custom-call | flops 536870912 | bytes 3424256 | tf_op jit(solution)/shard_map/pallas_call | solution.py:44
  78.4 4.4 %collective-permute-start.1 = (bf16[16,192,128]{2,1,0:T(8,128)(2,1)S(1)}, bf16[16,192,128]{2,1,0:T(8,128)(2,1)S(1)}, u32[]{:S(2)}, u32[]{:S(2)}) collective-permute-start(bf16[16,192,128]{2,1,0:T(8,128)(2,1)S(1)} %all_to_all.15.mine), channel_id=1, source_target_pairs={{0,32},{32,0},{64,96},{96,64},{128,160},{160,128},{192,224},{224,1... | collective-permute-start | bytes 2359304 | tf_op jit(solution)/shard_map/ppermute | solution.py:338
  82.8 12.1 %all-to-all-start.2 = ((f32[32,1,128]{2,1,0:T(1,128)}), f32[32,1,128]{2,1,0:T(1,128)S(1)}, u32[]{:S(2)}, u32[]{:S(2)}) async-start(f32[32,1,128]{2,1,0:T(1,128)} %get-tuple-element.27), calls=%async_computation.2 | async-start | bytes 32768 | tf_op jit(solution)/shard_map/all_to_all | solution.py:24
  94.9 0.0 collective-permute-done.1.other
  94.9 7.0 %shard_map.81 = (bf16[512,512]{1,0:T(8,128)(2,1)S(1)}, bf16[1024,512]{1,0:T(8,128)(2,1)}, f32[1,1,512,512]{3,2,1,0:T(8,128)}) custom-call(s32[32,2]{1,0:T(8,128)S(1)} %copy.8.owners, bf16[16,192,128]{2,1,0:T(8,128)(2,1)S(1)} %all_to_all.15.mine, bf16[16,192,128]{2,1,0:T(8,128)(2,1)S(1)} %collective-permute-done.1.other, ...), custom_call_target="tpu_custom_call" | custom-call | flops 2147483648 | bytes 9445632 | tf_op jit(solution)/shard_map/pallas_call | solution.py:44
  102.0 5.1 %all-to-all-done.2.own_every = f32[32,1,128]{2,1,0:T(1,128)S(1)} async-done(((f32[32,1,128]{2,1,0:T(1,128)}), f32[32,1,128]{2,1,0:T(1,128)S(1)}, u32[]{:S(2)}, u32[]{:S(2)}) %all-to-all-start.2) | async-done | bytes 16416 | tf_op jit(solution)/shard_map/all_to_all | solution.py:24
  107.1 3.3 %collective-permute-start.2 = (f32[32,1,128]{2,1,0:T(1,128)S(1)}, f32[32,1,128]{2,1,0:T(1,128)S(1)}, u32[]{:S(2)}, u32[]{:S(2)}) collective-permute-start(f32[32,1,128]{2,1,0:T(1,128)S(1)} %all-to-all-done.2.own_every), channel_id=1, source_target_pairs={{0,32},{32,0},{64,96},{96,64},{128,160},{160,128},{192,224},{224,1... | collective-permute-start | bytes 49160 | tf_op jit(solution)/shard_map/ppermute | solution.py:359
  110.4 0.8 collective-permute-done.2.other_every
  111.2 1.2 %shard_map.82 = bf16[1024,512]{1,0:T(8,128)(2,1)} custom-call(f32[32,1,128]{2,1,0:T(1,128)S(1)} %all-to-all-done.2.own_every, f32[32,1,128]{2,1,0:T(1,128)S(1)} %collective-permute-done.2.other_every, bf16[512,512]{1,0:T(8,128)(2,1)S(1)} %get-tuple-element.35.own, bf16[512,512]{1,0:T(8,128)(2,1)S(1)} %get-tuple-element.36.other), custom_call_target="tpu_custom_call" | custom-call | flops 1048576 | bytes 2129920 | tf_op jit(solution)/shard_map/pallas_call | solution.py:44
  (5 shorter events, 0.0 us)
Async XLA Ops:
  2.1 17.8 %collective-permute-start = (bf16[656,512]{1,0:T(8,128)(2,1)S(1)}, bf16[656,512]{1,0:T(8,128)(2,1)S(1)}, u32[]{:S(2)}, u32[]{:S(2)}) collective-permute-start(bf16[656,512]{1,0:T(8,128)(2,1)S(1)} %get-tuple-element.22), channel_id=1, source_target_pairs={{0,32},{32,0},{64,96},{96,64},{128,160},{160,128},{192,224},{224,1... | collective-permute-start | bytes 2015240 | tf_op jit(solution)/shard_map/ppermute | solution.py:308
  21.0 3.8 %copy-start.4 = (s32[32,2]{0,1:T(2,128)S(1)}, s32[32,2]{0,1:T(2,128)}, u32[]{:S(2)}) copy-start(s32[32,2]{0,1:T(2,128)} %param.9) | copy-start | bytes 772
  21.0 3.9 %copy-start = (bf16[1024,512]{1,0:T(8,128)(2,1)S(1)}, bf16[1024,512]{1,0:T(8,128)(2,1)}, u32[]{:S(2)}) copy-start(bf16[1024,512]{1,0:T(8,128)(2,1)} %left_hbm.1) | copy-start | bytes 3145732
  21.0 26.8 %all-to-all-start = ((bf16[16,200,128]{2,1,0:T(8,128)(2,1)}), bf16[16,200,128]{2,1,0:T(8,128)(2,1)S(1)}, u32[]{:S(2)}, u32[]{:S(2)}) async-start(bf16[16,200,128]{2,1,0:T(8,128)(2,1)} %shard_map.77), calls=%async_computation | async-start | bytes 1638400 | tf_op jit(solution)/shard_map/all_to_all | solution.py:24
  26.6 1.0 copy-start.2
  27.6 1.0 copy-start.3
  47.7 29.2 %copy-start.1 = (bf16[1024,512]{1,0:T(8,128)(2,1)S(1)}, bf16[1024,512]{1,0:T(8,128)(2,1)}, u32[]{:S(2)}) copy-start(bf16[1024,512]{1,0:T(8,128)(2,1)} %right_hbm.1) | copy-start | bytes 3145732
  78.4 16.5 %collective-permute-start.1 = (bf16[16,192,128]{2,1,0:T(8,128)(2,1)S(1)}, bf16[16,192,128]{2,1,0:T(8,128)(2,1)S(1)}, u32[]{:S(2)}, u32[]{:S(2)}) collective-permute-start(bf16[16,192,128]{2,1,0:T(8,128)(2,1)S(1)} %all_to_all.15.mine), channel_id=1, source_target_pairs={{0,32},{32,0},{64,96},{96,64},{128,160},{160,128},{192,224},{224,1... | collective-permute-start | bytes 2359304 | tf_op jit(solution)/shard_map/ppermute | solution.py:338
  82.8 24.3 %all-to-all-start.2 = ((f32[32,1,128]{2,1,0:T(1,128)}), f32[32,1,128]{2,1,0:T(1,128)S(1)}, u32[]{:S(2)}, u32[]{:S(2)}) async-start(f32[32,1,128]{2,1,0:T(1,128)} %get-tuple-element.27), calls=%async_computation.2 | async-start | bytes 32768 | tf_op jit(solution)/shard_map/all_to_all | solution.py:24
  107.1 4.1 %collective-permute-start.2 = (f32[32,1,128]{2,1,0:T(1,128)S(1)}, f32[32,1,128]{2,1,0:T(1,128)S(1)}, u32[]{:S(2)}, u32[]{:S(2)}) collective-permute-start(f32[32,1,128]{2,1,0:T(1,128)S(1)} %all-to-all-done.2.own_every), channel_id=1, source_target_pairs={{0,32},{32,0},{64,96},{96,64},{128,160},{160,128},{192,224},{224,1... | collective-permute-start | bytes 49160 | tf_op jit(solution)/shard_map/ppermute | solution.py:359

commit v5 on v3

--- a/solution.py
+++ b/solution.py
@@ -171,12 +171,44 @@
         squares[k] = filled
 
 
-def newton(owners, mine, other, diagonals, left_root, stats, squares, new_root, new_stats, grad, old_stats, sem):
+def powers(left_root, square, cube, square_buffer, cube_buffer, sems):
+    copies = []
+    for block in range(2):
+        rows = slice(block * WIDTH, (block + 1) * WIDTH)
+        left = left_root[rows, :]
+        second = mm(left, left).astype(BF16)
+        square_buffer[rows, :] = second
+        cube_buffer[rows, :] = mm(left, second).astype(BF16)
+        for k, (source, target) in enumerate(((square_buffer, square), (cube_buffer, cube))):
+            copies.append(pltpu.make_async_copy(source.at[rows], target.at[rows], sems.at[2 * block + k]))
+            copies[-1].start()
+    for copy in copies:
+        copy.wait()
+
+
+def newton(
+    owners, mine_hbm, other_hbm, diagonals, left_hbm, square_hbm, cube_hbm, stats, squares,
+    new_root, new_stats,
+    grad, left_root, square, cube, mine, other, old_stats, sems,
+):
     core = core_of()
     replica = lax.axis_index("dp")
     column = lax.axis_index("fsdp")
-    fetch = pltpu.make_async_copy(stats.at[0, 0], old_stats, sem)
-    fetch.start()
+    copies = [
+        pltpu.make_async_copy(source, target, sems.at[k])
+        for k, (source, target) in enumerate(
+            (
+                (mine_hbm, mine),
+                (other_hbm, other),
+                (stats.at[0, 0], old_stats),
+                (square_hbm, square),
+                (cube_hbm, cube),
+                (left_hbm, left_root),
+            )
+        )
+    ]
+    for copy in copies:
+        copy.start()
     owner_known = (owners[column, 0] == replica) | (owners[column, 1] == replica)
     row, col = row_col(HALF, HALF)
 
@@ -184,14 +216,17 @@
     def _():
         new_stats[...] = jnp.zeros_like(new_stats)
 
-    fetch.wait()
-
-    def one(block, source, first, second):
+    for copy in copies[:2]:
+        copy.wait()
+
+    def one(block, source, first, second, pending):
         rows = slice(block * WIDTH, (block + 1) * WIDTH)
         load_grad(source, grad)
         gram = lax.dot_general(
             grad[...], grad[...], (((1,), (1,)), ((), ())), preferred_element_type=F32
         )
+        for copy in pending:
+            copy.wait()
 
         @pl.when(owners[column, block] == replica)
         def _():
@@ -220,21 +255,18 @@
             [jnp.concatenate([high, corner], axis=1), jnp.concatenate([corner_t, low], axis=1)], axis=0
         )
         fresh = (BETA * old + (1.0 - BETA) * gram).astype(BF16)
-        left = left_root[rows, :]
-        square = mm(left, left).astype(BF16)
-        cube = mm(left, square).astype(BF16)
-        change = mm(cube, mm(fresh, square).astype(BF16))
-        new_root[rows, :] = (1.25 * left.astype(F32) - 0.25 * change).astype(BF16)
+        change = mm(cube[rows, :], mm(fresh, square[rows, :]).astype(BF16))
+        new_root[rows, :] = (1.25 * left_root[rows, :].astype(F32) - 0.25 * change).astype(BF16)
 
     @pl.when(core == 0)
     def _():
-        one(0, mine, mine, other)
-        one(1, other, mine, other)
+        one(0, mine, mine, other, copies[2:])
+        one(1, other, mine, other, [])
 
     @pl.when(core == 1)
     def _():
-        one(0, other, other, mine)
-        one(1, mine, other, mine)
+        one(0, other, other, mine, copies[2:])
+        one(1, mine, other, mine, [])
 
 
 def rescale(count):
@@ -281,6 +313,16 @@
     got = lax.ppermute(send, "dp", swap)
     (payload,) = call(pair_add, [keep, got], [shape((CHIPS, FIRST, TILE), BF16)], 1 << 20)
     arrived = exchange(payload, "dp", same_core)
+    whole = shape((rows, WIDTH), BF16)
+    square, cube = call(
+        powers,
+        [left_root],
+        [whole, whole],
+        4 * product,
+        [vmem((rows, WIDTH), BF16), vmem((rows, WIDTH), BF16), pltpu.SemaphoreType.DMA((4,))],
+        out_spaces=[pltpu.HBM, pltpu.HBM],
+    )
+    arrived, square, cube = lax.optimization_barrier((arrived, square, cube))
     repeated, diagonals = call(
         gather_sum,
         [owners, arrived],
@@ -305,13 +347,26 @@
         [block],
     )
     every = exchange(squares, "fsdp")
+    left_hbm, square, cube, mine_hbm, other_hbm = [
+        pltpu.with_memory_space_constraint(array, pltpu.HBM) for array in (left_root, square, cube, mine, other)
+    ]
+    table = vmem((rows, WIDTH), BF16)
     new_root, new_stats = call(
         newton,
-        [owners, mine, other, diagonals, left_root, stats, squares],
-        [shape((rows, WIDTH), BF16), shape((1, 1, WIDTH, WIDTH), F32)],
-        10 * product,
-        [block, vmem((WIDTH, WIDTH), F32), pltpu.SemaphoreType.DMA],
-        [pltpu.SMEM, vmem, vmem, vmem, vmem, pltpu.HBM, vmem],
+        [owners, mine_hbm, other_hbm, diagonals, left_hbm, square, cube, stats, squares],
+        [whole, shape((1, 1, WIDTH, WIDTH), F32)],
+        6 * product,
+        [
+            block,
+            table,
+            table,
+            table,
+            vmem((CHIPS, SECOND, TILE), BF16),
+            vmem((CHIPS, SECOND, TILE), BF16),
+            vmem((WIDTH, WIDTH), F32),
+            pltpu.SemaphoreType.DMA((6,)),
+        ],
+        [pltpu.SMEM, pltpu.HBM, pltpu.HBM, vmem] + [pltpu.HBM] * 4 + [vmem],
     )
     (update,) = call(
         rescale(float(rows * WIDTH * n_fsdp)),

time: 111 us -> 110 us (level)
  waiting for transfers between devices: 29.7 us -> 27.1 us
  Pallas kernels: 14 us -> 15.6 us
    all_to_all x2, waiting for transfers between devices: 26.9 us -> 24.4 us  [exchange(): return lax.all_to_all(array, axis, 0, 0, axis_index_groups=groups)]
    pallas_call x7 -> x8, Pallas kernels: 14 us -> 15.6 us  [call(): pl.pallas_call(body, out_shape=outs, in_specs=[pl.BlockSpec(memory_space=...]
  transfers between devices with their start and end apart: 4 -> 4, of which waited for: 4 -> 4; matrix products, arithmetic and copies ran while one was open for 0% -> 0% of each run, Pallas kernels for 7% -> 9%
where the time goes in v5:
time: 110 us
  starting transfers between devices  36.3 us (33%)
  blocking collectives  28.3 us (26%)
  waiting for transfers between devices  27.1 us (25%)
  Pallas kernels  15.6 us (14%)
  local copies, waits for them, and re-layouts  2.05 us (2%)
    all_to_all x1, blocking collectives, exchange(): return lax.all_to_all(array, axis, 0, 0, axis_index_groups=groups)  28.3 us
    all_to_all x2, waiting for transfers between devices, exchange(): return lax.all_to_all(array, axis, 0, 0, axis_index_groups=groups)  24.4 us
    ppermute x1, starting transfers between devices, local(): got = lax.ppermute(send, 'dp', swap)  16.1 us
    all_to_all x2, starting transfers between devices, exchange(): return lax.all_to_all(array, axis, 0, 0, axis_index_groups=groups)  15.8 us
    pallas_call x8, Pallas kernels, call(): pl.pallas_call(body, out_shape=outs, in_specs=[pl.BlockSpec(memory_space=...  15.6 us
    ppermute x1, starting transfers between devices, local(): other = lax.ppermute(mine, 'dp', swap)  4.41 us
  transfers between devices with their start and end apart: 4, of which 4 were waited for; matrix products, arithmetic and copies ran while one was open for 0% of the time, Pallas kernels for 9%

profile of v5, /device:TPU:1, one launch (start us, length us, event | category | flops | bytes accessed | tf_op | source)
XLA Modules:
  0.0 110.1 jit_solution(8313619134113260576)
XLA Ops:
  0.6 1.5 %shard_map.76 = (bf16[656,512]{1,0:T(8,128)(2,1)S(1)}, bf16[656,512]{1,0:T(8,128)(2,1)S(1)}) custom-call(bf16[1,1024,512]{2,1,0:T(8,128)(2,1)} %grads.1, f32[1,1,512,512]{3,2,1,0:T(8,128)} %stats.3), custom_call_target="tpu_custom_call" | custom-call | flops 1048576 | bytes 3440640 | tf_op jit(solution)/shard_map/pallas_call | solution.py:44
  2.1 16.1 %collective-permute-start = (bf16[656,512]{1,0:T(8,128)(2,1)S(1)}, bf16[656,512]{1,0:T(8,128)(2,1)S(1)}, u32[]{:S(2)}, u32[]{:S(2)}) collective-permute-start(bf16[656,512]{1,0:T(8,128)(2,1)S(1)} %get-tuple-element.19), channel_id=1, source_target_pairs={{0,32},{32,0},{64,96},{96,64},{128,160},{160,128},{192,224},{224,1... | collective-permute-start | bytes 2015240 | tf_op jit(solution)/shard_map/ppermute | solution.py:313
  18.2 1.7 %collective-permute-done.got = bf16[656,512]{1,0:T(8,128)(2,1)S(1)} collective-permute-done((bf16[656,512]{1,0:T(8,128)(2,1)S(1)}, bf16[656,512]{1,0:T(8,128)(2,1)S(1)}, u32[]{:S(2)}, u32[]{:S(2)}) %collective-permute-start) | collective-permute-done | bytes 671776 | tf_op jit(solution)/shard_map/ppermute | solution.py:313
  19.9 1.0 shard_map.77
  21.0 3.8 %all-to-all-start = ((bf16[16,200,128]{2,1,0:T(8,128)(2,1)}), bf16[16,200,128]{2,1,0:T(8,128)(2,1)S(1)}, u32[]{:S(2)}, u32[]{:S(2)}) async-start(bf16[16,200,128]{2,1,0:T(8,128)(2,1)} %shard_map.77), calls=%async_computation | async-start | bytes 1638400 | tf_op jit(solution)/shard_map/all_to_all | solution.py:24
  24.7 0.0 copy-done.6
  24.7 0.1 copy.8.owners
  24.8 1.8 %shard_map.78 = (bf16[1024,512]{1,0:T(8,128)(2,1)S(1)}, bf16[1024,512]{1,0:T(8,128)(2,1)S(1)}) custom-call(bf16[1024,512]{1,0:T(8,128)(2,1)S(1)} %copy-done.1), custom_call_target="tpu_custom_call" | custom-call | flops 1073741824 | bytes 3145728 | tf_op jit(solution)/shard_map/pallas_call | solution.py:44
  26.6 0.0 copy-start.4
  26.6 1.0 copy-done.4
  27.6 1.0 copy-done.5
  28.5 19.2 %all-to-all-done.got = bf16[16,200,128]{2,1,0:T(8,128)(2,1)S(1)} async-done(((bf16[16,200,128]{2,1,0:T(8,128)(2,1)}), bf16[16,200,128]{2,1,0:T(8,128)(2,1)S(1)}, u32[]{:S(2)}, u32[]{:S(2)}) %all-to-all-start) | async-done | bytes 819232 | tf_op jit(solution)/shard_map/all_to_all | solution.py:24
  47.7 0.9 shard_map.79
  48.7 28.3 %all_to_all.15.mine.mine_hbm = bf16[16,192,128]{2,1,0:T(8,128)(2,1)S(1)} all-to-all(bf16[16,192,128]{2,1,0:T(8,128)(2,1)S(1)} %get-tuple-element.23), channel_id=1, replica_groups={{0,64,128,192,256,320,384,448,512,576,640,704,768,832,896,960},{32,96,1..., dimensions={0} | all-to-all | bytes 1572864 | tf_op jit(solution)/shard_map/all_to_all | solution.py:24
  77.0 4.4 %collective-permute-start.1 = (bf16[16,192,128]{2,1,0:T(8,128)(2,1)S(1)}, bf16[16,192,128]{2,1,0:T(8,128)(2,1)S(1)}, u32[]{:S(2)}, u32[]{:S(2)}) collective-permute-start(bf16[16,192,128]{2,1,0:T(8,128)(2,1)S(1)} %all_to_all.15.mine.mine_hbm), channel_id=1, source_target_pairs={{0,32},{32,0},{64,96},{96,64},{128,160},{160,128},{192,224},{224,1... | collective-permute-start | bytes 2359304 | tf_op jit(solution)/shard_map/ppermute | solution.py:334
  81.4 0.0 copy-done
  81.4 0.9 shard_map.80
  82.2 1.0 collective-permute-done.1.other.other_hbm
  83.3 1.5 %shard_map.81 = (bf16[512,512]{1,0:T(8,128)(2,1)S(1)}, f32[32,1,128]{2,1,0:T(1,128)}) custom-call(bf16[16,192,128]{2,1,0:T(8,128)(2,1)S(1)} %collective-permute-done.1.other.other_hbm, bf16[1024,512]{1,0:T(8,128)(2,1)S(1)} %copy-done.1, bf16[1024,512]{1,0:T(8,128)(2,1)S(1)} %copy-done, f32[8,128]{1,0:T(8,128)S(1)} %get-tuple-element.24.own), custom_call_target="tpu_custom_call" | custom-call | flops 536870912 | bytes 3428352 | tf_op jit(solution)/shard_map/pallas_call | solution.py:44
  84.7 0.0 copy-done.3
  84.7 12.1 %all-to-all-start.2 = ((f32[32,1,128]{2,1,0:T(1,128)}), f32[32,1,128]{2,1,0:T(1,128)S(1)}, u32[]{:S(2)}, u32[]{:S(2)}) async-start(f32[32,1,128]{2,1,0:T(1,128)} %get-tuple-element.25.squares), calls=%async_computation.2 | async-start | bytes 32768 | tf_op jit(solution)/shard_map/all_to_all | solution.py:24
  96.8 6.9 %shard_map.83 = (bf16[1024,512]{1,0:T(8,128)(2,1)}, f32[1,1,512,512]{3,2,1,0:T(8,128)}) custom-call(s32[32,2]{1,0:T(8,128)S(1)} %copy.8.owners, bf16[16,192,128]{2,1,0:T(8,128)(2,1)} %copy-done.2, bf16[16,192,128]{2,1,0:T(8,128)(2,1)} %copy-done.3, f32[16,128]{1,0:T(8,128)S(1)} %get-tuple-element.28.diagonals, bf16[1024,512]{1,0:T(8,128)(2,1)} %left_hbm.1, ...), custom_call_target="tpu_custom_call" | custom-call | flops 1610612736 | bytes 7889152 | tf_op jit(solution)/shard_map/pallas_call | solution.py:44
  103.7 5.2 %all-to-all-done.2.every = f32[32,1,128]{2,1,0:T(1,128)S(1)} async-done(((f32[32,1,128]{2,1,0:T(1,128)}), f32[32,1,128]{2,1,0:T(1,128)S(1)}, u32[]{:S(2)}, u32[]{:S(2)}) %all-to-all-start.2) | async-done | bytes 16416 | tf_op jit(solution)/shard_map/all_to_all | solution.py:24
  108.9 1.2 %shard_map.82 = bf16[1024,512]{1,0:T(8,128)(2,1)} custom-call(f32[32,1,128]{2,1,0:T(1,128)S(1)} %all-to-all-done.2.every, bf16[512,512]{1,0:T(8,128)(2,1)S(1)} %get-tuple-element.26.own, bf16[512,512]{1,0:T(8,128)(2,1)S(1)} %get-tuple-element.27.other), custom_call_target="tpu_custom_call" | custom-call | flops 1048576 | bytes 2113536 | tf_op jit(solution)/shard_map/pallas_call | solution.py:44
  (8 shorter events, 0.0 us)
Async XLA Ops:
  2.1 17.8 %collective-permute-start = (bf16[656,512]{1,0:T(8,128)(2,1)S(1)}, bf16[656,512]{1,0:T(8,128)(2,1)S(1)}, u32[]{:S(2)}, u32[]{:S(2)}) collective-permute-start(bf16[656,512]{1,0:T(8,128)(2,1)S(1)} %get-tuple-element.19), channel_id=1, source_target_pairs={{0,32},{32,0},{64,96},{96,64},{128,160},{160,128},{192,224},{224,1... | collective-permute-start | bytes 2015240 | tf_op jit(solution)/shard_map/ppermute | solution.py:313
  21.0 3.8 %copy-start.6 = (s32[32,2]{0,1:T(2,128)S(1)}, s32[32,2]{0,1:T(2,128)}, u32[]{:S(2)}) copy-start(s32[32,2]{0,1:T(2,128)} %param.9) | copy-start | bytes 772
  21.0 3.9 %copy-start.1 = (bf16[1024,512]{1,0:T(8,128)(2,1)S(1)}, bf16[1024,512]{1,0:T(8,128)(2,1)}, u32[]{:S(2)}) copy-start(bf16[1024,512]{1,0:T(8,128)(2,1)} %left_hbm.1) | copy-start | bytes 3145732
  21.0 26.8 %all-to-all-start = ((bf16[16,200,128]{2,1,0:T(8,128)(2,1)}), bf16[16,200,128]{2,1,0:T(8,128)(2,1)S(1)}, u32[]{:S(2)}, u32[]{:S(2)}) async-start(bf16[16,200,128]{2,1,0:T(8,128)(2,1)} %shard_map.77), calls=%async_computation | async-start | bytes 1638400 | tf_op jit(solution)/shard_map/all_to_all | solution.py:24
  26.6 1.0 copy-start.4
  27.6 1.0 copy-start.5
  47.7 33.7 %copy-start = (bf16[1024,512]{1,0:T(8,128)(2,1)S(1)}, bf16[1024,512]{1,0:T(8,128)(2,1)}, u32[]{:S(2)}) copy-start(bf16[1024,512]{1,0:T(8,128)(2,1)} %right_root.3) | copy-start | bytes 3145732
  77.0 5.3 %copy-start.2 = (bf16[16,192,128]{2,1,0:T(8,128)(2,1)}, bf16[16,192,128]{2,1,0:T(8,128)(2,1)S(1)}, u32[]{:S(2)}) copy-start(bf16[16,192,128]{2,1,0:T(8,128)(2,1)S(1)} %all_to_all.15.mine.mine_hbm) | copy-start | bytes 2359300
  77.0 6.3 %collective-permute-start.1 = (bf16[16,192,128]{2,1,0:T(8,128)(2,1)S(1)}, bf16[16,192,128]{2,1,0:T(8,128)(2,1)S(1)}, u32[]{:S(2)}, u32[]{:S(2)}) collective-permute-start(bf16[16,192,128]{2,1,0:T(8,128)(2,1)S(1)} %all_to_all.15.mine.mine_hbm), channel_id=1, source_target_pairs={{0,32},{32,0},{64,96},{96,64},{128,160},{160,128},{192,224},{224,1... | collective-permute-start | bytes 2359304 | tf_op jit(solution)/shard_map/ppermute | solution.py:334
  83.3 1.5 %copy-start.3 = (bf16[16,192,128]{2,1,0:T(8,128)(2,1)}, bf16[16,192,128]{2,1,0:T(8,128)(2,1)S(1)}, u32[]{:S(2)}) copy-start(bf16[16,192,128]{2,1,0:T(8,128)(2,1)S(1)} %collective-permute-done.1.other.other_hbm) | copy-start | bytes 2359300
  84.7 24.2 %all-to-all-start.2 = ((f32[32,1,128]{2,1,0:T(1,128)}), f32[32,1,128]{2,1,0:T(1,128)S(1)}, u32[]{:S(2)}, u32[]{:S(2)}) async-start(f32[32,1,128]{2,1,0:T(1,128)} %get-tuple-element.25.squares), calls=%async_computation.2 | async-start | bytes 32768 | tf_op jit(solution)/shard_map/all_to_all | solution.py:24
